TPU v7x, 32 devices: a whole 2x2x4 slice. The times are simulated.
32 devices in a mesh: head: 2 (over core), blk: 16 (over z, y, x).
Axes of the slice: x: 2, y: 2, z: 4, core: 2. Of those that a mesh axis runs over, the one named last changes fastest.
Arguments:
- tokens: bfloat16 [4096, 1536], P(('head', 'blk')), may hold values from -6 to 6
- lengths: int32 [12], replicated, may hold values from 1 to 2048, 4096 in all
- expert_ids: int32 [4096, 2], P(('head', 'blk')), may hold values from 0 to 15, all different within a row; in each aligned block of 128 rows (0 to 127, 128 to 255, ...) at most 48 rows name the same one
- w_query: bfloat16 [1536, 1536], P(('head', 'blk')), may hold values from -0.15625 to 0.15625
- w_key: bfloat16 [1536, 512], P(('head', 'blk')), may hold values from -0.15625 to 0.15625
- w_value: bfloat16 [1536, 512], P(('head', 'blk')), may hold values from -0.15625 to 0.15625
- w_out: bfloat16 [1536, 1536], P(('head', 'blk')), may hold values from -2.5 to 2.5
- w_router: bfloat16 [1536, 16], P(('head', 'blk')), may hold values from -0.15625 to 0.15625
- gain_attn: bfloat16 [1536], P(('head', 'blk')), may hold values from 0.5 to 1.5
- gain_moe: bfloat16 [1536], P(('head', 'blk')), may hold values from 0.5 to 1.5
- w_gate: bfloat16 [16, 1536, 1024], P('blk', None, 'head'), may hold values from -0.15625 to 0.15625
- w_up: bfloat16 [16, 1536, 1024], P('blk', None, 'head'), may hold values from -0.15625 to 0.15625
- w_down: bfloat16 [16, 1024, 1536], P('blk', 'head'), may hold values from -0.1875 to 0.1875
- cotangent: bfloat16 [4096, 1536], P(('head', 'blk')), may hold values from -6 to 6
Outputs:
- output: bfloat16 [4096, 1536], P(('head', 'blk'))
- input_grad: bfloat16 [4096, 1536], P(('head', 'blk'))
- grad_query: float32 [1536, 1536], P(('head', 'blk'))
- grad_key: float32 [1536, 512], P(('head', 'blk'))
- grad_value: float32 [1536, 512], P(('head', 'blk'))
- grad_out: float32 [1536, 1536], P(('head', 'blk'))
- grad_router: float32 [1536, 16], P(('head', 'blk'))
- grad_gain_attn: float32 [1536], P(('head', 'blk'))
- grad_gain_moe: float32 [1536], P(('head', 'blk'))
- grad_gate: float32 [16, 1536, 1024], P('blk', None, 'head')
- grad_up: float32 [16, 1536, 1024], P('blk', None, 'head')
- grad_down: float32 [16, 1024, 1536], P('blk', 'head')
Inputs may be any that keep to these rules, and one draw needn't show every extreme that they name: The last entry counts the padding tokens at the end of the token order; the others are the documents' lengths in order; all entries add up to 4096. `expert_ids`: each token names two different experts. Among the 128 tokens of one device no expert is named by more than 48 tokens, and some expert reaches that bound.
All inputs are finite; a program needn't handle non-finite values.
Results may differ from a plain program's by a relative error of at most 0.025.
Values may be sent and summed in bfloat16 or wider, within the bound.
No kernel may reach another device: no remote copies, remote signals or barrier semaphores. Data moves between devices by JAX's collectives and lax.ppermute only.
A program may use at most 256 MiB of HBM per device.

v0:
```python
import math

import jax
import jax.numpy as jnp
from jax import lax
from jax.sharding import PartitionSpec as P

D = 1536
HQ = 24
HK = 8
HD = 64


EPS = 1e-05
NEG = -1e30


def for_sending(value):
    return jax.tree.map(lambda a: a.astype(jnp.bfloat16) if a.dtype == jnp.float32 else a, value)


def rms_scale(values):
    return lax.rsqrt(jnp.mean(values * values, axis=-1, keepdims=True) + EPS)


def doc_lookup(positions, seq_ends):
    return jnp.sum((positions[:, None] >= seq_ends[None, :]).astype(jnp.int32), axis=1)


def cycle_positions(whole_rows, tok_dev, head_count, blk_count):
    per_shard = head_count * tok_dev
    shard = whole_rows // per_shard
    inner = whole_rows % per_shard
    return inner // tok_dev * (blk_count * tok_dev) + shard * tok_dev + inner % tok_dev


def in_blocks(step_fn, carry, keys, values, start, width):
    total = keys.shape[0]
    if total <= width or total % width != 0:
        return step_fn(carry, keys, values, start)
    count = total // width
    key_blocks = keys.reshape((count, width) + keys.shape[1:])
    value_blocks = values.reshape((count, width) + values.shape[1:])

    def advance(state, item):
        number, key_part, value_part = item
        return (step_fn(state, key_part, value_part, start + number * width), None)

    carry, _ = lax.scan(
        advance, carry, (jnp.arange(count, dtype=jnp.int32), key_blocks, value_blocks)
    )
    return carry


def shards(
    tokens,
    lengths,
    expert_ids,
    w_query,
    w_key,
    w_value,
    w_out,
    w_router,
    gain_attn,
    gain_moe,
    w_gate,
    w_up,
    w_down,
    cotangent,
):
    f32 = jnp.float32
    bf16 = jnp.bfloat16
    head_count = lax.axis_size("head")
    blk_count = lax.axis_size("blk")
    tok_dev = tokens.shape[0]
    capacity = max(2, 3 * tok_dev // blk_count)
    hq_local = HQ // head_count
    hk_local = HK // head_count
    group = HQ // HK
    rows_here = head_count * tok_dev
    scale = 1.0 / math.sqrt(HD)
    seq_ends = jnp.cumsum(lengths)
    last_doc = lengths.shape[0] - 1
    blk_index = lax.axis_index("blk")
    own_pos = (lax.axis_index("head") * blk_count + blk_index) * tok_dev + jnp.arange(
        tok_dev, dtype=jnp.int32
    )
    valid_bool = doc_lookup(own_pos, seq_ends) < last_doc
    valid_float = valid_bool.astype(f32)[:, None]
    query_pos = cycle_positions(
        blk_index * rows_here + jnp.arange(rows_here, dtype=jnp.int32),
        tok_dev,
        head_count,
        blk_count,
    )
    query_doc = doc_lookup(query_pos, seq_ends)
    pair_experts = expert_ids.reshape(-1)
    live_pairs = jnp.repeat(valid_bool, 2)
    onehot = (
        (pair_experts[:, None] == jnp.arange(blk_count, dtype=jnp.int32)[None, :])
        & live_pairs[:, None]
    ).astype(jnp.int32)
    earlier = jnp.cumsum(onehot, axis=0) - onehot
    slot_index = jnp.sum(earlier * onehot, axis=1)
    kept_pairs = live_pairs & (slot_index < capacity)
    flat_index = pair_experts * capacity + slot_index
    slot_table = (
        (flat_index[None, :] == jnp.arange(blk_count * capacity, dtype=jnp.int32)[:, None])
        & kept_pairs[None, :]
    ).astype(bf16)
    pick_table = (
        expert_ids[:, :, None] == jnp.arange(blk_count, dtype=jnp.int32)[None, None, :]
    ).astype(f32)

    def allowed_for(start, count):
        key_pos = cycle_positions(
            start + jnp.arange(count, dtype=jnp.int32), tok_dev, head_count, blk_count
        )
        key_doc = doc_lookup(key_pos, seq_ends)
        return (query_doc[:, None] == key_doc[None, :]) & (key_pos[None, :] <= query_pos[:, None])

    def scores_for(q_grouped, key_part):
        return jnp.einsum("qhgd,khd->qhgk", q_grouped, key_part, preferred_element_type=f32) * scale

    def heads_layout(values):
        return jax.tree.map(
            lambda part, own: part.astype(own.dtype),
            lax.all_to_all(for_sending(values), "head", split_axis=1, concat_axis=0, tiled=True),
            values,
        )

    def token_layout(values):
        return jax.tree.map(
            lambda part, own: part.astype(own.dtype),
            lax.all_to_all(for_sending(values), "head", split_axis=0, concat_axis=1, tiled=True),
            values,
        )

    def to_owner(values):
        return (lax.all_to_all(values[0], "blk", split_axis=0, concat_axis=0, tiled=True),)

    def to_source(values):
        return (lax.all_to_all(values[0], "blk", split_axis=0, concat_axis=0, tiled=True),)

    def rows_of_pair(values):
        return (lax.all_gather(values[0], "head", axis=0, tiled=True),)

    def sum_of_pair(values):
        return (
            lax.psum_scatter(
                values[0].astype(jnp.bfloat16), "head", scatter_dimension=0, tiled=True
            ).astype(jnp.float32),
        )

    def forward():
        full_query, full_key, full_value, full_out, full_router, full_gain_attn, full_gain_moe = (
            lax.all_gather(w_query, ("head", "blk"), axis=0, tiled=True),
            lax.all_gather(w_key, ("head", "blk"), axis=0, tiled=True),
            lax.all_gather(w_value, ("head", "blk"), axis=0, tiled=True),
            lax.all_gather(w_out, ("head", "blk"), axis=0, tiled=True),
            lax.all_gather(w_router, ("head", "blk"), axis=0, tiled=True),
            lax.all_gather(gain_attn, ("head", "blk"), axis=0, tiled=True),
            lax.all_gather(gain_moe, ("head", "blk"), axis=0, tiled=True),
        )
        x_float = tokens.astype(f32)
        scale_one = rms_scale(x_float)
        normed_one = (x_float * scale_one * full_gain_attn.astype(f32)).astype(bf16)
        query = jnp.dot(normed_one, full_query, preferred_element_type=f32).astype(bf16)
        key = jnp.dot(normed_one, full_key, preferred_element_type=f32).astype(bf16)
        value = jnp.dot(normed_one, full_value, preferred_element_type=f32).astype(bf16)
        q_rows, k_rows, v_rows = heads_layout((query, key, value))
        q_grouped = q_rows.reshape(rows_here, hk_local, group, HD)
        k_heads = k_rows.reshape(rows_here, hk_local, HD)
        v_heads = v_rows.reshape(rows_here, hk_local, HD)

        def attend(state, key_part, value_part, start):
            allowed = allowed_for(start, key_part.shape[0])

            def attend_update(current):
                run_max, run_sum, run_acc = current
                mask = allowed[:, None, None, :]
                scores = jnp.where(mask, scores_for(q_grouped, key_part), NEG)
                new_max = jnp.maximum(run_max, jnp.max(scores, axis=-1))
                shrink = jnp.exp(run_max - new_max)
                weights = jnp.where(mask, jnp.exp(scores - new_max[..., None]), 0.0)
                new_sum = run_sum * shrink + jnp.sum(weights, axis=-1)
                new_acc = run_acc * shrink[..., None] + jnp.einsum(
                    "qhgk,khd->qhgd", weights.astype(bf16), value_part, preferred_element_type=f32
                )
                return (new_max, new_sum, new_acc)

            return lax.cond(jnp.any(allowed), attend_update, lambda current: current, state)

        start_state = (
            jnp.full((rows_here, hk_local, group), NEG, f32),
            jnp.zeros((rows_here, hk_local, group), f32),
            jnp.zeros((rows_here, hk_local, group, HD), f32),
        )
        run_max, run_sum, run_acc = in_blocks(
            attend,
            start_state,
            lax.all_gather(k_heads, "blk", axis=0, tiled=True),
            lax.all_gather(v_heads, "blk", axis=0, tiled=True),
            jnp.int32(0),
            rows_here,
        )
        log_total = run_max + jnp.log(run_sum)
        attn_rows = (run_acc / run_sum[..., None]).astype(bf16).reshape(rows_here, hq_local * HD)
        (attn_tokens,) = token_layout((attn_rows,))
        hidden_one = x_float + jnp.dot(attn_tokens, full_out, preferred_element_type=f32)
        scale_two = rms_scale(hidden_one)
        normed_two = (hidden_one * scale_two * full_gain_moe.astype(f32)).astype(bf16)
        logits = jnp.dot(normed_two, full_router, preferred_element_type=f32)
        mix_weights = jax.nn.softmax(jnp.sum(pick_table * logits[:, None, :], axis=2), axis=1)
        send_rows = (
            jnp.dot(slot_table, jnp.repeat(normed_two, 2, axis=0), preferred_element_type=f32)
            .astype(bf16)
            .reshape(blk_count, capacity, D)
        )
        (arrived,) = to_owner((send_rows,))
        (rows_all,) = rows_of_pair((arrived,))
        slot_rows = rows_all.reshape(-1, D)
        gate_mat = w_gate[0]
        up_mat = w_up[0]
        down_mat = w_down[0]
        gate_pre = jnp.dot(slot_rows, gate_mat, preferred_element_type=f32)
        up_pre = jnp.dot(slot_rows, up_mat, preferred_element_type=f32)
        inner_act = (jax.nn.silu(gate_pre) * up_pre).astype(bf16)
        partial_out = jnp.dot(inner_act, down_mat, preferred_element_type=f32)
        (summed,) = sum_of_pair((partial_out.reshape(rows_all.shape),))
        result = summed.astype(bf16)
        (returned,) = to_source((result,))
        y_pairs = jnp.einsum(
            "sj,sd->jd",
            slot_table,
            returned.reshape(blk_count * capacity, D),
            preferred_element_type=f32,
        ).reshape(tok_dev, 2, D)
        moe_part = jnp.sum(mix_weights[:, :, None] * y_pairs, axis=1)
        output = (valid_float * (hidden_one + moe_part)).astype(bf16)
        return dict(
            output=output,
            x_float=x_float,
            scale_one=scale_one,
            normed_one=normed_one,
            full_query=full_query,
            full_key=full_key,
            full_value=full_value,
            full_out=full_out,
            full_router=full_router,
            full_gain_attn=full_gain_attn,
            full_gain_moe=full_gain_moe,
            q_grouped=q_grouped,
            k_heads=k_heads,
            v_heads=v_heads,
            log_total=log_total,
            attn_rows=attn_rows,
            attn_tokens=attn_tokens,
            hidden_one=hidden_one,
            scale_two=scale_two,
            normed_two=normed_two,
            mix_weights=mix_weights,
            y_pairs=y_pairs,
            slot_rows=slot_rows,
            gate_pre=gate_pre,
            up_pre=up_pre,
            inner_act=inner_act,
            gate_mat=gate_mat,
            up_mat=up_mat,
            down_mat=down_mat,
        )

    saved = forward()
    output = saved["output"]
    saved = forward()
    d_out = cotangent.astype(f32) * valid_float
    mix_weights = saved["mix_weights"]
    d_mix = jnp.sum(d_out[:, None, :] * saved["y_pairs"], axis=2)
    d_y = (mix_weights[:, :, None] * d_out[:, None, :]).astype(bf16).reshape(2 * tok_dev, D)
    d_send = (
        jnp.dot(slot_table, d_y, preferred_element_type=f32)
        .astype(bf16)
        .reshape(blk_count, capacity, D)
    )
    (d_arrived,) = to_owner((d_send,))
    (d_rows,) = rows_of_pair((d_arrived,))
    d_flat = d_rows.reshape(-1, D)
    gate_pre = saved["gate_pre"]
    up_pre = saved["up_pre"]
    d_inner = jnp.einsum("rd,fd->rf", d_flat, saved["down_mat"], preferred_element_type=f32)
    sigmoid_gate = jax.nn.sigmoid(gate_pre)
    d_gate = (d_inner * up_pre * sigmoid_gate * (1.0 + gate_pre * (1.0 - sigmoid_gate))).astype(
        bf16
    )
    d_up = (d_inner * gate_pre * sigmoid_gate).astype(bf16)
    slot_rows = saved["slot_rows"]
    grad_gate_part = jnp.einsum("rd,rf->df", slot_rows, d_gate, preferred_element_type=f32)
    grad_up_part = jnp.einsum("rd,rf->df", slot_rows, d_up, preferred_element_type=f32)
    d_in_part = jnp.einsum(
        "rf,df->rd", d_gate, saved["gate_mat"], preferred_element_type=f32
    ) + jnp.einsum("rf,df->rd", d_up, saved["up_mat"], preferred_element_type=f32)
    (d_in_sum,) = sum_of_pair((d_in_part.reshape(d_rows.shape),))
    d_in = d_in_sum.astype(bf16)
    grad_gate = grad_gate_part[None]
    grad_up = grad_up_part[None]
    grad_down = jnp.einsum("rf,rd->fd", saved["inner_act"], d_flat, preferred_element_type=f32)[
        None
    ]
    (d_back,) = to_source((d_in,))
    d_pairs = jnp.einsum(
        "sj,sd->jd", slot_table, d_back.reshape(blk_count * capacity, D), preferred_element_type=f32
    ).reshape(tok_dev, 2, D)
    d_chosen = mix_weights * (d_mix - jnp.sum(mix_weights * d_mix, axis=1, keepdims=True))
    d_logits = jnp.sum(pick_table * d_chosen[:, :, None], axis=1).astype(bf16)
    normed_two = saved["normed_two"]
    grad_router = jnp.einsum("td,te->de", normed_two, d_logits, preferred_element_type=f32)
    d_normed_two = jnp.sum(d_pairs, axis=1) + jnp.einsum(
        "te,de->td", d_logits, saved["full_router"], preferred_element_type=f32
    )
    hidden_one = saved["hidden_one"]
    scale_two = saved["scale_two"]
    grad_gain_moe = jnp.sum(d_normed_two * hidden_one * scale_two, axis=0)
    along_two = saved["full_gain_moe"].astype(f32) * d_normed_two
    d_hidden = (
        d_out
        + scale_two * along_two
        - hidden_one
        * scale_two
        * scale_two
        * scale_two
        * jnp.mean(along_two * hidden_one, axis=-1, keepdims=True)
    )
    d_proj = d_hidden.astype(bf16)
    grad_out = jnp.einsum("ti,td->id", saved["attn_tokens"], d_proj, preferred_element_type=f32)
    d_attn = jnp.einsum("td,id->ti", d_proj, saved["full_out"], preferred_element_type=f32).astype(
        bf16
    )
    (d_attn_rows,) = heads_layout((d_attn,))
    d_attn_grouped = d_attn_rows.reshape(rows_here, hk_local, group, HD)
    attn_grouped = saved["attn_rows"].reshape(rows_here, hk_local, group, HD)
    row_dots = jnp.sum(d_attn_grouped.astype(f32) * attn_grouped.astype(f32), axis=-1)
    q_grouped = saved["q_grouped"]
    log_total = saved["log_total"]
    kv_width = hk_local * HD

    def probs_for(key_part, allowed):
        return jnp.where(
            allowed[:, None, None, :],
            jnp.exp(scores_for(q_grouped, key_part) - log_total[..., None]),
            0.0,
        )

    k_all, v_all = (
        lax.all_gather(for_sending(saved["k_heads"]), "blk", axis=0, tiled=True),
        lax.all_gather(for_sending(saved["v_heads"]), "blk", axis=0, tiled=True),
    )

    def query_grad(state, key_part, value_part, start):
        allowed = allowed_for(start, key_part.shape[0])

        def query_update(current):
            probs = probs_for(key_part, allowed)
            d_probs = jnp.einsum(
                "qhgd,khd->qhgk", d_attn_grouped, value_part, preferred_element_type=f32
            )
            d_scores = (probs * (d_probs - row_dots[..., None])).astype(bf16)
            return (
                current
                + jnp.einsum("qhgk,khd->qhgd", d_scores, key_part, preferred_element_type=f32)
                * scale
            )

        return lax.cond(jnp.any(allowed), query_update, lambda current: current, state)

    d_query = in_blocks(
        query_grad,
        jnp.zeros((rows_here, hk_local, group, HD), f32),
        k_all,
        v_all,
        0,
        rows_here * min(blk_count, 4),
    )

    def key_block(key_part, value_part, start):
        count = key_part.shape[0]
        allowed = allowed_for(start, count)

        def compute(unused):
            probs = probs_for(key_part, allowed)
            d_probs = jnp.einsum(
                "qhgd,khd->qhgk", d_attn_grouped, value_part, preferred_element_type=f32
            )
            d_scores = (probs * (d_probs - row_dots[..., None])).astype(bf16)
            d_key = (
                jnp.einsum("qhgk,qhgd->khd", d_scores, q_grouped, preferred_element_type=f32)
                * scale
            )
            d_value = jnp.einsum(
                "qhgk,qhgd->khd", probs.astype(bf16), d_attn_grouped, preferred_element_type=f32
            )
            return jnp.concatenate(
                [d_key.reshape(count, kv_width), d_value.reshape(count, kv_width)], axis=1
            )

        return lax.cond(
            jnp.any(allowed), compute, lambda unused: jnp.zeros((count, 2 * kv_width), f32), 0
        )

    count = lax.axis_size("blk") * rows_here
    key_part = lax.slice_in_dim(k_all, 0, count, axis=0)
    value_part = lax.slice_in_dim(v_all, 0, count, axis=0)
    number = count // rows_here
    parts = lax.map(
        lambda item: key_block(item[1], item[2], item[0] * rows_here),
        (
            jnp.arange(number, dtype=jnp.int32),
            key_part.reshape((number, rows_here) + key_part.shape[1:]),
            value_part.reshape((number, rows_here) + value_part.shape[1:]),
        ),
    )
    key_grads = lax.psum_scatter(
        parts.reshape(count, 2 * kv_width), "blk", scatter_dimension=0, tiled=True
    )
    d_query_rows = d_query.astype(bf16).reshape(rows_here, hq_local * HD)
    d_key_rows = key_grads[:, :kv_width].astype(bf16)
    d_value_rows = key_grads[:, kv_width:].astype(bf16)
    d_query_tok, d_key_tok, d_value_tok = token_layout((d_query_rows, d_key_rows, d_value_rows))
    normed_one = saved["normed_one"]
    grad_query = jnp.einsum("td,ti->di", normed_one, d_query_tok, preferred_element_type=f32)
    grad_key = jnp.einsum("td,ti->di", normed_one, d_key_tok, preferred_element_type=f32)
    grad_value = jnp.einsum("td,ti->di", normed_one, d_value_tok, preferred_element_type=f32)
    d_normed_one = (
        jnp.einsum("ti,di->td", d_query_tok, saved["full_query"], preferred_element_type=f32)
        + jnp.einsum("ti,di->td", d_key_tok, saved["full_key"], preferred_element_type=f32)
        + jnp.einsum("ti,di->td", d_value_tok, saved["full_value"], preferred_element_type=f32)
    )
    x_float = saved["x_float"]
    scale_one = saved["scale_one"]
    grad_gain_attn = jnp.sum(d_normed_one * x_float * scale_one, axis=0)
    along_one = saved["full_gain_attn"].astype(f32) * d_normed_one
    input_grad = (
        d_hidden
        + scale_one * along_one
        - x_float
        * scale_one
        * scale_one
        * scale_one
        * jnp.mean(along_one * x_float, axis=-1, keepdims=True)
    ).astype(bf16)
    (
        shard_query,
        shard_key,
        shard_value,
        shard_out,
        shard_router,
        shard_gain_attn,
        shard_gain_moe,
    ) = (
        lax.psum_scatter(grad_query, ("head", "blk"), scatter_dimension=0, tiled=True),
        lax.psum_scatter(grad_key, ("head", "blk"), scatter_dimension=0, tiled=True),
        lax.psum_scatter(grad_value, ("head", "blk"), scatter_dimension=0, tiled=True),
        lax.psum_scatter(grad_out, ("head", "blk"), scatter_dimension=0, tiled=True),
        lax.psum_scatter(grad_router, ("head", "blk"), scatter_dimension=0, tiled=True),
        lax.psum_scatter(grad_gain_attn, ("head", "blk"), scatter_dimension=0, tiled=True),
        lax.psum_scatter(grad_gain_moe, ("head", "blk"), scatter_dimension=0, tiled=True),
    )
    return (
        output,
        input_grad,
        shard_query,
        shard_key,
        shard_value,
        shard_out,
        shard_router,
        shard_gain_attn,
        shard_gain_moe,
        grad_gate,
        grad_up,
        grad_down,
    )


def solution(mesh):
    placed = (
        P(("head", "blk"), None),
        P(),
        P(("head", "blk"), None),
        P(("head", "blk"), None),
        P(("head", "blk"), None),
        P(("head", "blk"), None),
        P(("head", "blk"), None),
        P(("head", "blk"), None),
        P(("head", "blk")),
        P(("head", "blk")),
        P("blk", None, "head"),
        P("blk", None, "head"),
        P("blk", "head", None),
        P(("head", "blk"), None),
    )
    return jax.shard_map(
        shards,
        mesh=mesh,
        in_specs=placed,
        out_specs=(
            P(("head", "blk"), None),
            P(("head", "blk"), None),
            P(("head", "blk"), None),
            P(("head", "blk"), None),
            P(("head", "blk"), None),
            P(("head", "blk"), None),
            P(("head", "blk"), None),
            P(("head", "blk")),
            P(("head", "blk")),
            P("blk", None, "head"),
            P("blk", None, "head"),
            P("blk", "head", None),
        ),
        check_vma=False,
    )
```

profile of v0, /device:TPU:0, one launch (start us, length us, event | category | flops | bytes accessed | tf_op | source)
XLA Modules:
  0.0 1646.1 jit_solution(11861667711151069691)
XLA Ops:
  10.5 42.1 %all-reduce.5 = (bf16[1536]{0:T(1024)(128)(2,1)S(1)}, bf16[1536]{0:T(1024)(128)(2,1)S(1)}) all-reduce(bf16[1536]{0:T(1024)(128)(2,1)S(1)} %dynamic-update-slice, bf16[1536]{0:T(1024)(128)(2,1)S(1)} %dynamic-update-slice.1), channel_id=1, replica_groups=mesh['head'=2,'blk'=16] {'head','blk'}, use_global_device_ids=true, to_apply=%add | all-reduce | flops 3072 | bytes 12288
  53.7 14.9 all-gather.10.cloned.1.call-done
  75.5 49.8 %all-gather.16.cloned.1.call-done = bf16[1536,512]{1,0:T(8,128)(2,1)} async-done(((bf16[48,512]{1,0:T(8,128)(2,1)}), bf16[1536,512]{1,0:T(8,128)(2,1)}) %all-gather.16.cloned.1.call-update) | async-done | bytes 1572880 | tf_op jit(solution)/shard_map/all_gather | solution.py:159
  135.5 56.8 %all-gather.12.cloned.1.call-done = bf16[4096,4,64]{0,2,1:T(8,128)(2,1)} async-done(((bf16[256,4,64]{0,2,1:T(8,128)(2,1)}), bf16[4096,4,64]{0,2,1:T(8,128)(2,1)}) %all-gather.12.cloned.1.call-update) | async-done | bytes 2097168 | tf_op jit(solution)/shard_map/all_gather | solution.py:202
  195.5 63.1 %all-gather.18.cloned.1.call-done = bf16[4096,4,64]{0,2,1:T(8,128)(2,1)} async-done(((bf16[256,4,64]{0,2,1:T(8,128)(2,1)}), bf16[4096,4,64]{0,2,1:T(8,128)(2,1)}) %all-gather.18.cloned.1.call-update) | async-done | bytes 2097168 | tf_op jit(solution)/shard_map/all_gather | solution.py:203
  261.9 61.5 %all-gather.14.cloned.1.call-done = bf16[1536,1536]{1,0:T(8,128)(2,1)} async-done(((bf16[48,1536]{1,0:T(8,128)(2,1)}), bf16[1536,1536]{1,0:T(8,128)(2,1)}) %all-gather.14.cloned.1.call-update) | async-done | bytes 4718608 | tf_op jit(solution)/shard_map/all_gather | solution.py:157
  331.4 105.2 %while.55 = (s32[]{:T(128)}, f32[256,4,3]{0,2,1:T(4,128)S(1)}, f32[256,4,3]{0,2,1:T(4,128)S(1)}, f32[256,4,3,64]{0,3,2,1:T(8,128)S(1)}, s32[256]{0:T(256)S(1)}, ...) while((s32[]{:T(128)}, f32[256,4,3]{0,2,1:T(4,128)S(1)}, ...), condition=%wide.region_11.12_spmd.clone, body=%wide.region_4.11_spmd.clone.sunk | while | flops 212242688 | bytes 12133715 | solution.py:49
  354.0 4.3 conditional.9
  375.4 4.3 conditional.9
  389.6 4.3 conditional.9
  403.8 4.3 conditional.9
  418.1 4.3 conditional.9
  432.3 4.3 conditional.9
  440.4 4.8 all_to_all.185
  456.5 11.5 all-to-all-start.4
  474.1 75.9 %all-gather = bf16[32,48,16]{1,2,0:T(8,128)(2,1)S(1)} all-gather(bf16[1,48,16]{1,2,0:T(8,128)(2,1)S(1)} %bitcast.364), channel_id=1, replica_groups=mesh['head'=2,'blk'=16] {'head','blk'}, dimensions={0}, use_global_device_ids=true | all-gather | bytes 50688 | tf_op jit(solution)/shard_map/all_gather | solution.py:161
  552.9 33.4 %all_to_all.186 = bf16[16,24,1536]{2,1,0:T(8,128)(2,1)} all-to-all(bf16[16,24,1536]{2,1,0:T(8,128)(2,1)S(1)} %bitcast.335), channel_id=1, replica_groups=mesh['head'=2,'blk'=16] {'blk'}, dimensions={0} | all-to-all | bytes 2359296 | tf_op jit(solution)/shard_map/all_to_all | solution.py:140
  586.4 4.8 fusion.111
  594.9 5.6 multiply_convert_fusion
  609.3 7.4 reduce-scatter.13.cloned.1.call-done
  616.8 6.9 all-to-all-start.7
  623.7 7.2 reduce-scatter.11.cloned.1.call-done
  630.9 19.9 %all-to-all-done.7 = bf16[16,24,1536]{2,1,0:T(8,128)(2,1)S(1)} async-done(((bf16[16,24,1536]{2,1,0:T(8,128)(2,1)}), bf16[16,24,1536]{2,1,0:T(8,128)(2,1)S(1)}, u32[]{:S(2)}, u32[]{:S(2)}) %all-to-all-start.7) | async-done | bytes 1179680 | tf_op jit(solution)/shard_map/all_to_all | solution.py:143
  650.8 7.0 all-to-all-start.5
  660.1 23.5 %all-to-all-done.5 = bf16[16,24,1536]{2,1,0:T(8,128)(2,1)} async-done(((bf16[16,24,1536]{2,1,0:T(8,128)(2,1)}), bf16[16,24,1536]{2,1,0:T(8,128)(2,1)}, u32[]{:S(2)}, u32[]{:S(2)}) %all-to-all-start.5) | async-done | bytes 1179680 | tf_op jit(solution)/shard_map/all_to_all | solution.py:143
  689.5 4.4 all_to_all.187
  694.7 154.3 %while.57 = (s32[]{:T(128)}, f32[16,256,512]{2,1,0:T(8,128)}, s32[256]{0:T(256)S(1)}, s32[16]{0:T(128)S(1)}, s32[12]{0:T(128)S(1)}, /*index=5*/bf16[16,256,4,64]...) while((s32[]{:T(128)}, f32[16,256,512]{2,1,0:T(8,128)}, ...), condition=%wide.region_39.40_spmd.clone, body=%wide.region_34.39_spmd.clone.sunk | while | flops 411007232 | bytes 27768648 | solution.py:413
  697.5 6.6 conditional.11
  715.8 6.6 conditional.11
  726.2 6.6 conditional.11
  736.7 6.6 conditional.11
  747.1 6.6 conditional.11
  757.6 6.6 conditional.11
  768.1 6.6 conditional.11
  778.5 6.6 conditional.11
  789.0 6.6 conditional.11
  799.4 6.6 conditional.11
  809.9 6.6 conditional.11
  820.4 6.6 conditional.11
  830.9 6.6 conditional.11
  841.4 6.6 conditional.11
  854.0 82.6 %while.56 = (s32[]{:T(128)}, f32[256,4,3,64]{0,3,2,1:T(8,128)S(1)}, s32[256]{0:T(256)S(1)}, s32[4]{0:T(128)S(1)}, s32[12]{0:T(128)S(1)}, /*index=5*/bf16[4,1024,...) while((s32[]{:T(128)}, f32[256,4,3,64]{0,3,2,1:T(8,128)S(1)}, ...), condition=%wide.region_33.34_spmd.clone, body=%wide.region_28.33_spmd.clone.sunk | while | flops 1228366592 | bytes 29672244 | solution.py:49
  857.3 17.5 %conditional.10 = (f32[256,4,3,64]{0,3,2,1:T(8,128)S(1)}) conditional(s32[]{:T(128)} %convert_element_type.341, f32[256,4,3,64]{0,3,2,1:T(8,128)S(1)} %get-tuple-element.1591, (pred[256,1024]{0,1:T(8,128)(4,1)S(1)}, bf16[4,1024,4,64]{1,3,2,0:T(8,128)(2,1)}, s32[]{:T(128)}, bf16[256,4,3,64]{0,3,2,1:T(8,128)(2,1)S(1)}, f32[256,4,3]{0,2,1:T(4,128)S(1)}, ...), branch_computations={%region_31.31_spmd, %region_32.32_spmd} | conditional | flops 1227227136 | bytes 29386248 | solution.py:373
  857.3 7.4 fusion.49
  864.8 10.1 fusion.43
  878.2 17.2 %conditional.10 = (f32[256,4,3,64]{0,3,2,1:T(8,128)S(1)}) conditional(s32[]{:T(128)} %convert_element_type.341, f32[256,4,3,64]{0,3,2,1:T(8,128)S(1)} %get-tuple-element.1591, (pred[256,1024]{0,1:T(8,128)(4,1)S(1)}, bf16[4,1024,4,64]{1,3,2,0:T(8,128)(2,1)}, s32[]{:T(128)}, bf16[256,4,3,64]{0,3,2,1:T(8,128)(2,1)S(1)}, f32[256,4,3]{0,2,1:T(4,128)S(1)}, ...), branch_computations={%region_31.31_spmd, %region_32.32_spmd} | conditional | flops 1227227136 | bytes 29386248 | solution.py:373
  878.2 7.5 fusion.49
  885.7 9.7 fusion.43
  898.8 17.2 %conditional.10 = (f32[256,4,3,64]{0,3,2,1:T(8,128)S(1)}) conditional(s32[]{:T(128)} %convert_element_type.341, f32[256,4,3,64]{0,3,2,1:T(8,128)S(1)} %get-tuple-element.1591, (pred[256,1024]{0,1:T(8,128)(4,1)S(1)}, bf16[4,1024,4,64]{1,3,2,0:T(8,128)(2,1)}, s32[]{:T(128)}, bf16[256,4,3,64]{0,3,2,1:T(8,128)(2,1)S(1)}, f32[256,4,3]{0,2,1:T(4,128)S(1)}, ...), branch_computations={%region_31.31_spmd, %region_32.32_spmd} | conditional | flops 1227227136 | bytes 29386248 | solution.py:373
  898.8 7.4 fusion.49
  906.2 9.7 fusion.43
  919.3 17.3 %conditional.10 = (f32[256,4,3,64]{0,3,2,1:T(8,128)S(1)}) conditional(s32[]{:T(128)} %convert_element_type.341, f32[256,4,3,64]{0,3,2,1:T(8,128)S(1)} %get-tuple-element.1591, (pred[256,1024]{0,1:T(8,128)(4,1)S(1)}, bf16[4,1024,4,64]{1,3,2,0:T(8,128)(2,1)}, s32[]{:T(128)}, bf16[256,4,3,64]{0,3,2,1:T(8,128)(2,1)S(1)}, f32[256,4,3]{0,2,1:T(4,128)S(1)}, ...), branch_computations={%region_31.31_spmd, %region_32.32_spmd} | conditional | flops 1227227136 | bytes 29386248 | solution.py:373
  919.3 7.5 fusion.49
  926.8 9.8 fusion.43
  942.7 5.1 fusion.161
  949.0 5.0 fusion.133
  954.1 84.0 %reduce-scatter.15.cloned.1.call-done = f32[256,512]{1,0:T(8,128)} async-done(((f32[4096,512]{1,0:T(8,128)}), f32[256,512]{1,0:T(8,128)}) %reduce-scatter.15.cloned.1.call-update) | async-done | bytes 524304 | tf_op jit(solution)/shard_map/reduce_scatter | solution.py:421
  1053.1 4.9 convolution_bitcast_fusion.2
  1066.9 74.9 %reduce-scatter.25.cloned.1.call-done = f32[48,16]{1,0:T(8,128)} async-done(((f32[1536,16]{1,0:T(8,128)}), f32[48,16]{1,0:T(8,128)}) %reduce-scatter.25.cloned.1.call-update) | async-done | bytes 3088
  1148.7 40.3 %all-reduce.4 = (f32[1536]{0:T(1024)S(1)}, f32[1536]{0:T(1024)S(1)}) all-reduce(f32[1536]{0:T(1024)S(1)} %get-tuple-element.1189, f32[1536]{0:T(1024)S(1)} %get-tuple-element.1185), channel_id=10, replica_groups=mesh['head'=2,'blk'=16] {'head','blk'}, use_global_device_ids=true, to_apply=%region_48.49.clone | all-reduce | flops 3072 | bytes 24576
  1192.3 91.4 %reduce-scatter.17.cloned.1.call-done = f32[48,1536]{1,0:T(8,128)} async-done(((f32[1536,1536]{1,0:T(8,128)}), f32[48,1536]{1,0:T(8,128)}) %reduce-scatter.17.cloned.1.call-update) | async-done | bytes 294928 | tf_op jit(solution)/shard_map/reduce_scatter | solution.py:459
  1283.7 141.5 %reduce-scatter.23.cloned.1.call-done = f32[48,1536]{1,0:T(8,128)} async-done(((f32[1536,1536]{1,0:T(8,128)}), f32[48,1536]{1,0:T(8,128)}) %reduce-scatter.23.cloned.1.call-update) | async-done | bytes 294928 | tf_op jit(solution)/shard_map/reduce_scatter | solution.py:462
  1425.2 106.9 %reduce-scatter.19.cloned.1.call-done = f32[48,512]{1,0:T(8,128)} async-done(((f32[1536,512]{1,0:T(8,128)}), f32[48,512]{1,0:T(8,128)}) %reduce-scatter.19.cloned.1.call-update) | async-done | bytes 98320 | tf_op jit(solution)/shard_map/reduce_scatter | solution.py:460
  1532.1 107.1 %reduce-scatter.21.cloned.1.call-done = f32[48,512]{1,0:T(8,128)} async-done(((f32[1536,512]{1,0:T(8,128)}), f32[48,512]{1,0:T(8,128)}) %reduce-scatter.21.cloned.1.call-update) | async-done | bytes 98320 | tf_op jit(solution)/shard_map/reduce_scatter | solution.py:461
  (591 shorter events, 385.6 us)
Async XLA Ops:
  7.2 587.7 %copy-start = (bf16[1,512,1536]{2,1,0:T(8,128)(2,1)S(1)}, bf16[1,512,1536]{2,1,0:T(8,128)(2,1)}, u32[]{:S(2)}) copy-start(bf16[1,512,1536]{2,1,0:T(8,128)(2,1)} %param.38) | copy-start | bytes 4718596
  7.2 118.2 %copy-start.3 = (bf16[128,1536]{1,0:T(8,128)(2,1)S(1)}, bf16[128,1536]{1,0:T(8,128)(2,1)}, u32[]{:S(2)}) copy-start(bf16[128,1536]{1,0:T(8,128)(2,1)} %param.26) | copy-start | bytes 1179652
  7.2 61.4 %all-gather.10.cloned.1.call-start = ((), (), s32[]{:S(2)}) async-start(), calls=%async_computation.20 | async-start | bytes 1622016 | tf_op jit(solution)/shard_map/all_gather | solution.py:158
  7.9 117.4 %all-gather.16.cloned.1.call-start = ((), (), s32[]{:S(2)}) async-start(), calls=%async_computation.23 | async-start | bytes 1622016 | tf_op jit(solution)/shard_map/all_gather | solution.py:159
  8.7 183.6 %all-gather.12.cloned.1.call-start = ((), (), s32[]{:S(2)}) async-start(), calls=%async_computation.21 | async-start | bytes 2228224 | tf_op jit(solution)/shard_map/all_gather | solution.py:202
  70.6 62.7 %copy-start.22 = (s32[128,2]{0,1:T(2,128)S(1)}, s32[128,2]{0,1:T(2,128)}, u32[]{:S(2)}) copy-start(s32[128,2]{0,1:T(2,128)} %param.28) | copy-start | bytes 3076
  70.7 62.9 %copy-start.27 = (s32[12]{0:T(128)S(1)}, s32[12]{0:T(128)}, u32[]{:S(2)}) copy-start(s32[12]{0:T(128)} %param.27) | copy-start | bytes 148
  75.4 183.2 %all-gather.18.cloned.1.call-start = ((), (), s32[]{:S(2)}) async-start(), calls=%async_computation.24 | async-start | bytes 2228224 | tf_op jit(solution)/shard_map/all_gather | solution.py:203
  132.0 191.3 %all-gather.14.cloned.1.call-start = ((), (), s32[]{:S(2)}) async-start(), calls=%async_computation.22 | async-start | bytes 4866048 | tf_op jit(solution)/shard_map/all_gather | solution.py:157
  132.6 312.6 %all-gather.20.cloned.1.call-start = ((), (), s32[]{:S(2)}) async-start(), calls=%async_computation.25 | async-start | bytes 4866048 | tf_op jit(solution)/shard_map/all_gather | solution.py:160
  436.6 12.0 copy-start.9
  453.8 14.4 copy-start.17
  456.5 94.3 %all-to-all-start.4 = ((bf16[16,24,1536]{2,1,0:T(8,128)(2,1)}), bf16[16,24,1536]{2,1,0:T(8,128)(2,1)}, u32[]{:S(2)}, u32[]{:S(2)}) async-start(bf16[16,24,1536]{2,1,0:T(8,128)(2,1)} %bitcast.334), calls=%async_computation.4 | async-start | bytes 2359296 | tf_op jit(solution)/shard_map/all_to_all | solution.py:140
  468.0 118.3 %all-gather.22.cloned.1.call-start = ((), (), s32[]{:S(2)}) async-start(), calls=%async_computation.26 | async-start | bytes 3538944 | tf_op jit(solution)/shard_map/all_gather | solution.py:146
  469.3 4.8 copy-start.23
  550.9 44.0 %all-gather.24.cloned.1.call-start = ((), (), s32[]{:S(2)}) async-start(), calls=%async_computation.28 | async-start | bytes 3538944 | tf_op jit(solution)/shard_map/all_gather | solution.py:146
  586.3 30.5 %reduce-scatter.13.cloned.1.call-start = ((), (), s32[]{:S(2)}) async-start(), calls=%async_computation.29 | async-start | bytes 3538944 | tf_op jit(solution)/shard_map/reduce_scatter | solution.py:150
  586.4 4.8 copy-start.15
  586.4 4.8 copy-start.24
  594.9 5.6 copy-start.26
  600.5 1.4 copy-start.28
  600.5 1.4 copy-start.20
  600.5 2.0 copy-start.16
  605.3 25.5 %reduce-scatter.11.cloned.1.call-start = ((), (), s32[]{:S(2)}) async-start(), calls=%async_computation.27 | async-start | bytes 3538944 | tf_op jit(solution)/shard_map/reduce_scatter | solution.py:150
  616.8 34.0 %all-to-all-start.7 = ((bf16[16,24,1536]{2,1,0:T(8,128)(2,1)}), bf16[16,24,1536]{2,1,0:T(8,128)(2,1)S(1)}, u32[]{:S(2)}, u32[]{:S(2)}) async-start(bf16[16,24,1536]{2,1,0:T(8,128)(2,1)} %reduce-scatter.13.cloned.1.call-done), calls=%async_computation.9 | async-start | bytes 2359296 | tf_op jit(solution)/shard_map/all_to_all | solution.py:143
  650.8 7.3 copy-start.11
  650.8 37.1 %slice-start.2 = ((s8[4718592]{0:T(1024)(128)(4,1)}), s8[524288]{0:T(1024)(128)(4,1)S(1)}, s32[]{:S(2)}) async-start(s8[4718592]{0:T(1024)(128)(4,1)} %bitcast.321), calls=%async_computation.38 | async-start | bytes 1048576
  650.8 32.9 %all-to-all-start.5 = ((bf16[16,24,1536]{2,1,0:T(8,128)(2,1)}), bf16[16,24,1536]{2,1,0:T(8,128)(2,1)}, u32[]{:S(2)}, u32[]{:S(2)}) async-start(bf16[16,24,1536]{2,1,0:T(8,128)(2,1)} %reduce-scatter.11.cloned.1.call-done), calls=%async_computation.6 | async-start | bytes 2359296 | tf_op jit(solution)/shard_map/all_to_all | solution.py:143
  657.8 380.4 %reduce-scatter.15.cloned.1.call-start = ((), (), s32[]{:S(2)}) async-start(), calls=%async_computation.30 | async-start | bytes 8912896 | tf_op jit(solution)/shard_map/reduce_scatter | solution.py:421
  658.1 28.1 %copy-start.5 = (f32[128,1536]{1,0:T(8,128)S(1)}, f32[128,1536]{1,0:T(8,128)}, u32[]{:S(2)}) copy-start(f32[128,1536]{1,0:T(8,128)} %copy-done.4) | copy-start | bytes 2359300
  683.6 3.0 copy-start.18
  683.6 4.2 slice-start.3
  687.8 1.7 copy-start.6
  689.5 5.1 copy-start.10
  699.1 1.7 copy-start.2
  717.3 1.7 copy-start.2
  727.8 1.7 copy-start.2
  738.2 1.7 copy-start.2
  748.7 1.7 copy-start.2
  759.1 1.7 copy-start.2
  769.6 1.7 copy-start.2
  780.1 1.7 copy-start.2
  790.5 1.7 copy-start.2
  801.0 1.7 copy-start.2
  811.4 1.7 copy-start.2
  822.0 1.7 copy-start.2
  832.5 1.7 copy-start.2
  842.9 1.7 copy-start.2
  849.1 3.3 copy-start.8
  937.6 5.1 all-to-all-start.9
  941.0 200.8 %reduce-scatter.25.cloned.1.call-start = ((), (), s32[]{:S(2)}) async-start(), calls=%async_computation.35 | async-start | bytes 811008
  942.3 341.4 %reduce-scatter.17.cloned.1.call-start = ((), (), s32[]{:S(2)}) async-start(), calls=%async_computation.31 | async-start | bytes 9732096 | tf_op jit(solution)/shard_map/reduce_scatter | solution.py:459
  947.8 1.2 copy-start.12
  947.8 477.4 %reduce-scatter.23.cloned.1.call-start = ((), (), s32[]{:S(2)}) async-start(), calls=%async_computation.34 | async-start | bytes 9732096 | tf_op jit(solution)/shard_map/reduce_scatter | solution.py:462
  954.1 578.0 %reduce-scatter.19.cloned.1.call-start = ((), (), s32[]{:S(2)}) async-start(), calls=%async_computation.32 | async-start | bytes 3244032 | tf_op jit(solution)/shard_map/reduce_scatter | solution.py:460
  1045.6 593.6 %reduce-scatter.21.cloned.1.call-start = ((), (), s32[]{:S(2)}) async-start(), calls=%async_computation.33 | async-start | bytes 3244032 | tf_op jit(solution)/shard_map/reduce_scatter | solution.py:461
  1051.9 1.1 copy-start.29
  1053.1 4.9 copy-start.21
  1053.1 4.9 copy-start.25
  1053.1 11.2 slice-start
  1058.0 3.1 copy-start.14
  1058.0 3.1 copy-start.19
  1058.0 6.2 slice-start.1
  1143.2 496.0 %copy-start.1 = (bf16[1,512,1536]{2,1,0:T(8,128)(2,1)S(1)}, bf16[1,512,1536]{2,1,0:T(8,128)(2,1)}, u32[]{:S(2)}) copy-start(bf16[1,512,1536]{2,1,0:T(8,128)(2,1)} %param.38) | copy-start | bytes 4718596
  (3 other events, 2.9 us)
Sparse Core Ops, SparseCore 0:
  10.9 57.6 all-gather.9
  71.5 53.8 all-gather.15
  128.6 63.6 all-gather.11
  195.5 63.1 all-gather.17
  261.4 61.8 all-gather.13
  326.1 61.8 all-gather.19
  551.0 9.1 all-gather.21
  586.4 8.3 all-gather.23
  605.4 11.2 reduce-scatter.12
  619.4 11.3 reduce-scatter.10
  849.2 188.9 reduce-scatter.14
  1043.1 98.6 reduce-scatter.24
  1148.3 135.3 reduce-scatter.16
  1290.0 135.1 reduce-scatter.22
  1431.0 101.0 reduce-scatter.18
  1537.9 101.1 reduce-scatter.20
where the time goes:
time: 1660 us; the launch traced here: 1650 us
  waiting for transfers between devices  914 us (55%)
  matrix products  274 us (17%)
  blocking collectives  220 us (13%)
  local copies, waits for them, and re-layouts  89.9 us (5%)
  other arithmetic  53.8 us (3%)
  loops' own time  49.3 us (3%)
  starting transfers between devices  29.9 us (2%)
    reduce_scatter x1, waiting for transfers between devices, shards(): lax.psum_scatter(grad_out, ('head', 'blk'), scatter_dimension=0, tiled=True)  142 us
    reduce_scatter x1, waiting for transfers between devices, shards(): lax.psum_scatter(grad_value, ('head', 'blk'), scatter_dimension=0, tiled=...  107 us
    reduce_scatter x1, waiting for transfers between devices, shards(): lax.psum_scatter(grad_key, ('head', 'blk'), scatter_dimension=0, tiled=True)  107 us
    reduce_scatter x1, waiting for transfers between devices, shards(): lax.psum_scatter(grad_query, ('head', 'blk'), scatter_dimension=0, tiled=...  91.4 us
    reduce_scatter x1, waiting for transfers between devices, shards(): lax.psum_scatter(parts.reshape(count, 2 * kv_width), 'blk', scatter_dimen...  84 us
    unnamed x2, blocking collectives  82.4 us
    unnamed x17, waiting for transfers between devices  77.5 us
    all_gather x1, blocking collectives, forward(): lax.all_gather(w_router, ('head', 'blk'), axis=0, tiled=True)  75.9 us
  transfers between devices with their start and end apart: 20, of which 17 were waited for; matrix products, arithmetic and copies ran while one was open for 15% of the time, Pallas kernels for 0%

commit v1 on v0

v1 whole, which is shorter than its diff:
```python
import functools

import jax
import jax.numpy as jnp
from jax import lax
from jax.experimental import pallas as pl
from jax.experimental.pallas import tpu as pltpu
from jax.sharding import Mesh
from jax.sharding import PartitionSpec as P

D = 1536
HQ = 24
HK = 8
HD = 64
GROUP = HQ // HK
QW = GROUP * HD
KV = 2 * HD
QKV = QW + KV
LANE = 128
EPS = 1e-05
NEG = -1e30
BQ = 256
F32 = jnp.float32
BF16 = jnp.bfloat16

PLANE = ("head", "hg")
BLK = ("tg", "hg")
ALL = ("head", "tg", "hg")


def pad_up(count):
    return -(-count // LANE) * LANE


def rms_scale(values):
    return lax.rsqrt(jnp.mean(values * values, axis=-1, keepdims=True) + EPS)


def doc_ranges(lengths_ref, segments, q_pos, first, key_rows):
    start = jnp.zeros_like(q_pos)
    low = jnp.int32(0)
    end = jnp.int32(0)
    for j in range(segments):
        end = end + lengths_ref[j]
        start = jnp.where(q_pos >= end, end, start)
        low = jnp.where(first >= end, end, low)
    return start, low // key_rows


def block_place(meta_ref, step, steps, run, tokens_all):
    half = steps // 2
    return (step // half) * (tokens_all // 2) + meta_ref[0] * run + (step % half) * BQ


def head_rows(ref, h, shift):
    part = ref[:, h * HD : (h + 1) * HD]
    zero = jnp.zeros_like(part)
    return jnp.concatenate([zero, part] if shift else [part, zero], axis=1)


def dot_nt(a, b):
    return lax.dot_general(a, b, (((1,), (1,)), ((), ())), preferred_element_type=F32)


def dot_tn(a, b):
    return lax.dot_general(a, b, (((0,), (0,)), ((), ())), preferred_element_type=F32)


def attend_kernel(lengths_ref, meta_ref, q_ref, kv_ref, o_ref, lse_ref, *, segments, planes):
    step = pl.program_id(0)
    steps = pl.num_programs(0)
    rows = kv_ref.shape[1]
    tokens_all = kv_ref.shape[0] * rows
    first = block_place(meta_ref, step, steps, rows, tokens_all)
    q_pos = first + lax.broadcasted_iota(jnp.int32, (1, BQ), 1)
    start, low = doc_ranges(lengths_ref, segments, q_pos, first, rows)
    high = (first + BQ - 1) // rows + 1
    heads = [head_rows(q_ref, h, False) * jnp.asarray(HD**-0.5, BF16) for h in range(GROUP)]

    def visit(block, state):
        part = kv_ref[(block % planes) * 2 + block // planes]
        k_pos = block * rows + lax.broadcasted_iota(jnp.int32, (rows, BQ), 0)
        mask = (k_pos >= start) & (k_pos <= q_pos)
        values = part[:, HD:]
        out = []
        for h in range(GROUP):
            run_max, run_sum, acc = state[h]
            scores = jnp.where(mask, dot_nt(part, heads[h]), NEG)
            new_max = jnp.maximum(run_max, jnp.max(scores, axis=0, keepdims=True))
            shrink = jnp.exp(run_max - new_max)
            weights = jnp.exp(scores - new_max)
            new_sum = run_sum * shrink + jnp.sum(weights, axis=0, keepdims=True)
            acc = acc * shrink + dot_tn(values, weights.astype(BF16))
            out.append((new_max, new_sum, acc))
        return tuple(out)

    begin = tuple(
        (
            jnp.full((1, BQ), NEG, F32),
            jnp.zeros((1, BQ), F32),
            jnp.zeros((HD, BQ), F32),
        )
        for _ in range(GROUP)
    )
    state = lax.fori_loop(low, high, visit, begin)
    o_ref[...] = jnp.concatenate([acc / total for _, total, acc in state], axis=0).T.astype(BF16)
    lse_ref[0] = jnp.concatenate([top + jnp.log(total) for top, total, _ in state], axis=0)


def attend_back_kernel(
    lengths_ref,
    meta_ref,
    q_ref,
    do_ref,
    o_ref,
    lse_ref,
    kv_ref,
    dq_ref,
    dkv_ref,
    acc_ref,
    *,
    segments,
    planes,
):
    step = pl.program_id(0)
    steps = pl.num_programs(0)
    rows = kv_ref.shape[1]
    tokens_all = kv_ref.shape[0] * rows
    first = block_place(meta_ref, step, steps, rows, tokens_all)
    q_pos = first + lax.broadcasted_iota(jnp.int32, (1, BQ), 1)
    start, low = doc_ranges(lengths_ref, segments, q_pos, first, rows)
    high = (first + BQ - 1) // rows + 1
    scale = HD**-0.5

    @pl.when(step == 0)
    def _():
        acc_ref[...] = jnp.zeros_like(acc_ref)

    queries = [head_rows(q_ref, h, False) * jnp.asarray(scale, BF16) for h in range(GROUP)]
    d_outs = [head_rows(do_ref, h, True) for h in range(GROUP)]
    products = (do_ref[...].astype(F32) * o_ref[...].astype(F32)).T
    row_dots = [
        jnp.sum(products[h * HD : (h + 1) * HD], axis=0, keepdims=True) for h in range(GROUP)
    ]
    both = [jnp.concatenate([queries[h], d_outs[h]], axis=0) for h in range(GROUP)]

    def visit(block, state):
        place = (block % planes) * 2 + block // planes
        part = kv_ref[place]
        k_pos = block * rows + lax.broadcasted_iota(jnp.int32, (rows, BQ), 0)
        mask = (k_pos >= start) & (k_pos <= q_pos)
        keys = part[:, :HD]
        total = jnp.zeros((rows, KV), F32)
        out = []
        for h in range(GROUP):
            scores = dot_nt(part, queries[h])
            probs = jnp.where(mask, jnp.exp(scores - lse_ref[0, h : h + 1, :]), 0.0)
            d_probs = dot_nt(part, d_outs[h])
            d_scores = (probs * (d_probs - row_dots[h])).astype(BF16)
            total = total + jnp.dot(
                jnp.concatenate([d_scores, probs.astype(BF16)], axis=1),
                both[h],
                preferred_element_type=F32,
            )
            out.append(state[h] + dot_tn(keys, d_scores))
        acc_ref[place] += total
        return tuple(out)

    begin = tuple(jnp.zeros((HD, BQ), F32) for _ in range(GROUP))
    state = lax.fori_loop(low, high, visit, begin)
    dq_ref[...] = (jnp.concatenate(state, axis=0) * scale).T.astype(BF16)

    @pl.when(step == steps - 1)
    def _():
        dkv_ref[...] = acc_ref[...].astype(BF16)


def attend(lengths, meta, query, kv_blocks, planes):
    rows = query.shape[0]
    steps = rows // BQ
    return pl.pallas_call(
        functools.partial(attend_kernel, segments=lengths.shape[0], planes=planes),
        out_shape=(
            jax.ShapeDtypeStruct((rows, QW), BF16),
            jax.ShapeDtypeStruct((steps, GROUP, BQ), F32),
        ),
        grid_spec=pltpu.PrefetchScalarGridSpec(
            num_scalar_prefetch=2,
            grid=(steps,),
            in_specs=[
                pl.BlockSpec((BQ, QW), lambda i, *_: (i, 0)),
                pl.BlockSpec(kv_blocks.shape, lambda i, *_: (0, 0, 0)),
            ],
            out_specs=[
                pl.BlockSpec((BQ, QW), lambda i, *_: (i, 0)),
                pl.BlockSpec((1, GROUP, BQ), lambda i, *_: (i, 0, 0)),
            ],
        ),
        name="attend",
    )(lengths, meta, query, kv_blocks)


def attend_back(lengths, meta, query, d_out, out, lse, kv_blocks, planes):
    rows = query.shape[0]
    steps = rows // BQ
    return pl.pallas_call(
        functools.partial(attend_back_kernel, segments=lengths.shape[0], planes=planes),
        out_shape=(
            jax.ShapeDtypeStruct((rows, QW), BF16),
            jax.ShapeDtypeStruct(kv_blocks.shape, BF16),
        ),
        grid_spec=pltpu.PrefetchScalarGridSpec(
            num_scalar_prefetch=2,
            grid=(steps,),
            in_specs=[
                pl.BlockSpec((BQ, QW), lambda i, *_: (i, 0)),
                pl.BlockSpec((BQ, QW), lambda i, *_: (i, 0)),
                pl.BlockSpec((BQ, QW), lambda i, *_: (i, 0)),
                pl.BlockSpec((1, GROUP, BQ), lambda i, *_: (i, 0, 0)),
                pl.BlockSpec(kv_blocks.shape, lambda i, *_: (0, 0, 0)),
            ],
            out_specs=[
                pl.BlockSpec((BQ, QW), lambda i, *_: (i, 0)),
                pl.BlockSpec(kv_blocks.shape, lambda i, *_: (0, 0, 0)),
            ],
            scratch_shapes=[pltpu.VMEM(kv_blocks.shape, F32)],
        ),
        name="attend_back",
    )(lengths, meta, query, d_out, out, lse, kv_blocks)


def split_float(value):
    high = value.astype(BF16)
    return high, (value - high.astype(F32)).astype(BF16)


def shards(
    tokens,
    lengths,
    expert_ids,
    w_query,
    w_key,
    w_value,
    w_out,
    w_router,
    gain_attn,
    gain_moe,
    w_gate,
    w_up,
    w_down,
    cotangent,
):
    heads = lax.axis_size("head")
    planes = lax.axis_size("tg")
    members = lax.axis_size("hg")
    blk_count = planes * members
    devices = heads * blk_count
    in_group = heads * members
    tok_dev = tokens.shape[0]
    rows_dev = w_query.shape[0]
    experts = blk_count
    capacity = max(2, 3 * tok_dev // experts)
    slots = experts * capacity
    rows_group = in_group * tok_dev
    run = members * tok_dev
    slab = pad_up(QKV + experts + 1)
    plane = lax.axis_index("tg")
    blk_index = plane * members + lax.axis_index("hg")
    partner = [(i, heads - 1 - i) for i in range(heads)]

    by_group = jnp.concatenate(
        [
            w_query.reshape(rows_dev, in_group, QW),
            w_key.reshape(rows_dev, in_group, HD),
            w_value.reshape(rows_dev, in_group, HD),
            jnp.broadcast_to(gain_attn[:, None, None], (rows_dev, in_group, 1)),
            jnp.zeros((rows_dev, in_group, slab - QKV - 1), BF16),
        ],
        axis=2,
    )
    to_send = by_group.transpose(1, 0, 2).reshape(heads, 1, members, rows_dev, slab)
    to_send = jnp.broadcast_to(to_send, (heads, planes, members, rows_dev, slab))
    own_slab = lax.all_to_all(
        to_send.reshape(devices, rows_dev, slab), ALL, split_axis=0, concat_axis=0, tiled=True
    ).reshape(D, slab)
    x_group = lax.all_gather(tokens, PLANE, axis=0, tiled=True)
    extra = pad_up(experts + 1)
    out_shard = jnp.concatenate(
        [
            w_out,
            w_router,
            gain_moe[:, None],
            jnp.zeros((rows_dev, extra - experts - 1), BF16),
        ],
        axis=1,
    )
    full_out = lax.all_gather(out_shard, ALL, axis=0, tiled=True)
    full_in = lax.all_gather(by_group.reshape(rows_dev, in_group * slab), ALL, axis=0, tiled=True)

    seq_ends = jnp.cumsum(lengths)
    own_pos = (lax.axis_index("head") * blk_count + blk_index) * tok_dev + jnp.arange(
        tok_dev, dtype=jnp.int32
    )
    valid_bool = own_pos < seq_ends[-2]
    valid_float = valid_bool.astype(F32)[:, None]
    pair_experts = expert_ids.reshape(-1)
    live_pairs = jnp.repeat(valid_bool, 2)
    onehot = (
        (pair_experts[:, None] == jnp.arange(experts, dtype=jnp.int32)[None, :])
        & live_pairs[:, None]
    ).astype(jnp.int32)
    earlier = jnp.cumsum(onehot, axis=0) - onehot
    slot_index = jnp.sum(earlier * onehot, axis=1)
    kept_pairs = live_pairs & (slot_index < capacity)
    flat_index = jnp.where(kept_pairs, pair_experts * capacity + slot_index, -1)
    slot_ids = jnp.arange(slots, dtype=jnp.int32)
    slot_bool = flat_index[None, :] == slot_ids[:, None]
    token_index = flat_index.reshape(tok_dev, 2)
    token_table = (
        (token_index[:, 0][:, None] == slot_ids[None, :])
        | (token_index[:, 1][:, None] == slot_ids[None, :])
    ).astype(BF16)
    pick_table = (
        expert_ids[:, :, None] == jnp.arange(experts, dtype=jnp.int32)[None, None, :]
    ).astype(F32)

    def to_experts(rows):
        sent = lax.all_to_all(
            rows.reshape(experts, capacity, rows.shape[1]),
            BLK,
            split_axis=0,
            concat_axis=0,
            tiled=True,
        ).reshape(slots, rows.shape[1])
        return jnp.concatenate([sent, lax.ppermute(sent, "head", partner)], axis=0)

    def to_tokens(partial):
        theirs = lax.ppermute(partial[slots:].astype(BF16), "head", partner)
        summed = (partial[:slots] + theirs.astype(F32)).astype(BF16)
        return lax.all_to_all(
            summed.reshape(experts, capacity, summed.shape[1]),
            BLK,
            split_axis=0,
            concat_axis=0,
            tiled=True,
        ).reshape(slots, summed.shape[1])

    def pick_rows(values):
        return lax.dot_general(
            token_table, values, (((0,), (0,)), ((), ())), preferred_element_type=F32
        )

    x_float = x_group.astype(F32)
    gain_one = own_slab[:, QKV].astype(F32)[None, :]
    normed_one = (x_float * rms_scale(x_float) * gain_one).astype(BF16)
    qkv = jnp.dot(normed_one, own_slab, preferred_element_type=F32).astype(BF16)
    query = qkv[:, :QW]
    kv_own = qkv[:, QW:QKV]
    kv_blocks = lax.all_gather(kv_own, "tg", axis=0, tiled=True).reshape(planes * 2, run, KV)
    meta = plane.astype(jnp.int32).reshape(1)
    attn_rows, lse = attend(lengths, meta, query, kv_blocks, planes)
    attn_tokens = lax.all_to_all(attn_rows, PLANE, split_axis=0, concat_axis=1, tiled=True)

    d_rows = to_experts(pick_rows(cotangent).astype(BF16))

    own_x = tokens.astype(F32)
    hidden_one = own_x + jnp.dot(attn_tokens, full_out[:, :D], preferred_element_type=F32)
    scale_two = rms_scale(hidden_one)
    gain_two = full_out[:, D + experts].astype(F32)[None, :]
    router = full_out[:, D : D + experts]
    normed_two = (hidden_one * scale_two * gain_two).astype(BF16)
    logits = jnp.dot(normed_two, router, preferred_element_type=F32)
    mix = jax.nn.softmax(jnp.sum(pick_table * logits[:, None, :], axis=2), axis=1)
    slot_mix = jnp.sum(jnp.where(slot_bool, mix.reshape(1, -1), 0.0), axis=1, keepdims=True)
    mix_high, mix_low = split_float(slot_mix)
    moe_rows = to_experts(
        jnp.concatenate(
            [
                pick_rows(normed_two).astype(BF16),
                mix_high,
                mix_low,
                jnp.zeros((slots, LANE - 2), BF16),
            ],
            axis=1,
        )
    )

    gate_mat = w_gate[0]
    up_mat = w_up[0]
    down_mat = w_down[0]
    rows = moe_rows[:, :D]
    row_mix = moe_rows[:, D : D + 1].astype(F32) + moe_rows[:, D + 1 : D + 2].astype(F32)
    gate_pre = jnp.dot(rows, gate_mat, preferred_element_type=F32)
    up_pre = jnp.dot(rows, up_mat, preferred_element_type=F32)
    sigmoid_gate = jax.nn.sigmoid(gate_pre)
    inner = gate_pre * sigmoid_gate * up_pre
    inner_act = inner.astype(BF16)
    d_inner = jnp.einsum("rd,fd->rf", d_rows, down_mat, preferred_element_type=F32)
    d_mix_part = jnp.sum(d_inner * inner, axis=1, keepdims=True)
    d_scaled = d_inner * row_mix
    d_gate = (d_scaled * up_pre * sigmoid_gate * (1.0 + gate_pre * (1.0 - sigmoid_gate))).astype(
        BF16
    )
    d_up = (d_scaled * gate_pre * sigmoid_gate).astype(BF16)
    d_in = jnp.einsum("rf,df->rd", d_gate, gate_mat, preferred_element_type=F32) + jnp.einsum(
        "rf,df->rd", d_up, up_mat, preferred_element_type=F32
    )
    mix_part_high, mix_part_low = split_float(d_mix_part)
    d_back = to_tokens(
        jnp.concatenate(
            [
                d_in,
                mix_part_high.astype(F32),
                mix_part_low.astype(F32),
                jnp.zeros((2 * slots, LANE - 2), F32),
            ],
            axis=1,
        )
    )
    y_back = to_tokens(jnp.dot(inner_act, down_mat, preferred_element_type=F32) * row_mix)
    output = (
        valid_float * (hidden_one + jnp.dot(token_table, y_back, preferred_element_type=F32))
    ).astype(BF16)
    d_y = (d_rows.astype(F32) * row_mix).astype(BF16)
    grad_gate = jnp.einsum("rd,rf->df", rows, d_gate, preferred_element_type=F32)[None]
    grad_up = jnp.einsum("rd,rf->df", rows, d_up, preferred_element_type=F32)[None]
    grad_down = jnp.einsum("rf,rd->fd", inner_act, d_y, preferred_element_type=F32)[None]

    d_out = cotangent.astype(F32) * valid_float
    slot_d_mix = d_back[:, D : D + 1].astype(F32) + d_back[:, D + 1 : D + 2].astype(F32)
    d_mix = jnp.sum(jnp.where(slot_bool, slot_d_mix, 0.0), axis=0).reshape(tok_dev, 2)
    d_chosen = mix * (d_mix - jnp.sum(mix * d_mix, axis=1, keepdims=True))
    d_logits = jnp.sum(pick_table * d_chosen[:, :, None], axis=1).astype(BF16)
    grad_router_part = jnp.einsum("td,te->de", normed_two, d_logits, preferred_element_type=F32)
    d_normed_two = jnp.dot(
        token_table, d_back[:, :D], preferred_element_type=F32
    ) + jnp.einsum("te,de->td", d_logits, router, preferred_element_type=F32)
    gain_moe_part = jnp.sum(d_normed_two * hidden_one * scale_two, axis=0)
    along_two = gain_two * d_normed_two
    d_hidden = (
        d_out
        + scale_two * along_two
        - hidden_one
        * (
            scale_two
            * scale_two
            * scale_two
            * jnp.mean(along_two * hidden_one, axis=-1, keepdims=True)
        )
    )
    d_proj = d_hidden.astype(BF16)
    d_attn = jnp.einsum("td,id->ti", d_proj, full_out[:, :D], preferred_element_type=F32).astype(
        BF16
    )
    d_attn_rows = lax.all_to_all(d_attn, PLANE, split_axis=1, concat_axis=0, tiled=True)
    grad_out_part = jnp.einsum("ti,td->id", attn_tokens, d_proj, preferred_element_type=F32)
    grad_out = lax.psum_scatter(
        grad_out_part.astype(BF16), ALL, scatter_dimension=0, tiled=True
    ).astype(F32)

    d_query, d_kv_blocks = attend_back(
        lengths, meta, query, d_attn_rows, attn_rows, lse, kv_blocks, planes
    )
    d_kv_parts = lax.all_to_all(
        d_kv_blocks.reshape(planes, rows_group, KV), "tg", split_axis=0, concat_axis=0, tiled=True
    )
    d_kv = jnp.sum(d_kv_parts.astype(F32), axis=0).astype(BF16)
    d_qkv = jnp.concatenate(
        [d_query, d_kv, jnp.zeros((rows_group, slab - QKV), BF16)], axis=1
    )
    d_tokens = lax.all_to_all(d_qkv, PLANE, split_axis=0, concat_axis=1, tiled=True)
    grad_in = jnp.einsum("td,ti->di", normed_one, d_qkv, preferred_element_type=F32)
    grad_in = jnp.concatenate(
        [
            grad_in[:, :QKV],
            grad_router_part,
            gain_moe_part[:, None],
            jnp.zeros((D, slab - QKV - experts - 1), F32),
        ],
        axis=1,
    ).astype(BF16)
    grad_parts = lax.all_to_all(
        grad_in.reshape(devices, rows_dev, slab), ALL, split_axis=0, concat_axis=0, tiled=True
    ).astype(F32)
    grad_small = jnp.sum(grad_parts[:, :, QKV:], axis=0)
    grad_router = grad_small[:, :experts]
    grad_gain_moe = grad_small[:, experts]
    grad_qkv = jnp.sum(
        grad_parts[:, :, :QKV].reshape(heads, planes, members, rows_dev, QKV), axis=1
    )
    grad_qkv = grad_qkv.reshape(in_group, rows_dev, QKV).transpose(1, 0, 2)
    grad_query = grad_qkv[:, :, :QW].reshape(rows_dev, HQ * HD)
    grad_key = grad_qkv[:, :, QW : QW + HD].reshape(rows_dev, HK * HD)
    grad_value = grad_qkv[:, :, QW + HD :].reshape(rows_dev, HK * HD)
    grad_gain_attn = (
        jnp.sum(grad_qkv * by_group[:, :, :QKV].astype(F32), axis=(1, 2)) / gain_attn.astype(F32)
    )
    d_normed_one = jnp.einsum("ti,di->td", d_tokens, full_in, preferred_element_type=F32)
    scale_one = rms_scale(own_x)
    along_one = gain_one * d_normed_one
    input_grad = (
        d_hidden
        + scale_one * along_one
        - own_x
        * (
            scale_one
            * scale_one
            * scale_one
            * jnp.mean(along_one * own_x, axis=-1, keepdims=True)
        )
    ).astype(BF16)
    return (
        output,
        input_grad,
        grad_query,
        grad_key,
        grad_value,
        grad_out,
        grad_router,
        grad_gain_attn,
        grad_gain_moe,
        grad_gate,
        grad_up,
        grad_down,
    )


def solution(mesh):
    heads = mesh.shape["head"]
    members = HK // heads
    planes = mesh.shape["blk"] // members
    inner = Mesh(mesh.devices.reshape(heads, planes, members), ALL)
    rows = P(ALL, None)
    placed = (
        rows,
        P(),
        rows,
        rows,
        rows,
        rows,
        rows,
        rows,
        P(ALL),
        P(ALL),
        P(BLK, None, "head"),
        P(BLK, None, "head"),
        P(BLK, "head", None),
        rows,
    )
    return jax.shard_map(
        shards,
        mesh=inner,
        in_specs=placed,
        out_specs=(
            rows,
            rows,
            rows,
            rows,
            rows,
            rows,
            rows,
            P(ALL),
            P(ALL),
            P(BLK, None, "head"),
            P(BLK, None, "head"),
            P(BLK, "head", None),
        ),
        check_vma=False,
    )
```

time: 1660 us -> 574 us (0.35)
  waiting for transfers between devices: 914 us -> 236 us
  matrix products: 274 us -> 66.2 us
  blocking collectives: 220 us -> 85 us
  loops' own time: 49.3 us -> 0 us
  local copies, waits for them, and re-layouts: 89.9 us -> 53.5 us
  Pallas kernels: 0 us -> 35.9 us
  other arithmetic: 53.8 us -> 29.1 us
    reduce_scatter x7 -> x1, waiting for transfers between devices: 546 us -> 25.3 us  [shards(): lax.psum_scatter(grad_out_part.astype(BF16), ALL, scatter_dimension=0, ti...]
    dot_general x105 -> x22, matrix products: 273 us -> 66.2 us  [the longest x1 7.29 us: shards(): jnp.einsum('ti,di->td', d_tokens, full_in, preferred_element_type=F32)]
    all_gather x8 -> x4, waiting for transfers between devices: 247 us -> 62 us  [the longest x1 36.3 us: shards(): full_out = lax.all_gather(out_shard, ALL, axis=0, tiled=True)]
    all_to_all x4 -> x8, waiting for transfers between devices: 43.5 us -> 146 us  [the longest x2 79.4 us: to_experts(): lax.all_to_all(rows.reshape(experts, capacity, rows.shape[1]), BLK, split...]
    unnamed x2 -> x0, blocking collectives: 82.4 us -> none
    unnamed x17 -> x5, waiting for transfers between devices: 77.5 us -> 0.75 us
    all_gather x1 -> x0, blocking collectives: 75.9 us -> none  [forward(): lax.all_gather(w_router, ('head', 'blk'), axis=0, tiled=True)]
    another operation x39 -> x0, loops' own time: 49.3 us -> none  [the longest x2 26.7 us: in_blocks(): lax.scan(advance, carry, (jnp.arange(count, dtype=jnp.int32), key_blocks,...]
  transfers between devices with their start and end apart: 20 -> 17, of which waited for: 17 -> 13; matrix products, arithmetic and copies ran while one was open for 15% -> 24% of each run, Pallas kernels for 0% -> 6%
where the time goes in v1:
time: 574 us; the launch traced here: 565 us
  waiting for transfers between devices  236 us (41%)
  blocking collectives  85 us (15%)
  matrix products  66.2 us (12%)
  local copies, waits for them, and re-layouts  53.5 us (9%)
  starting transfers between devices  43.4 us (8%)
  Pallas kernels  35.9 us (6%)
  other arithmetic  29.1 us (5%)
  between operations  15.4 us (3%)
    all_to_all x2, waiting for transfers between devices, to_experts(): lax.all_to_all(rows.reshape(experts, capacity, rows.shape[1]), BLK, split...  79.4 us
    all_to_all x1, blocking collectives, to_tokens(): lax.all_to_all(summed.reshape(experts, capacity, summed.shape[1]), BLK, s...  47 us
    all_to_all x1, blocking collectives, shards(): lax.all_to_all(to_send.reshape(devices, rows_dev, slab), ALL, split_axis=...  38 us
    all_gather x1, waiting for transfers between devices, shards(): full_out = lax.all_gather(out_shard, ALL, axis=0, tiled=True)  36.3 us
    reduce_scatter x1, waiting for transfers between devices, shards(): lax.psum_scatter(grad_out_part.astype(BF16), ALL, scatter_dimension=0, ti...  25.3 us
    all_to_all x1, waiting for transfers between devices, shards(): lax.all_to_all(grad_in.reshape(devices, rows_dev, slab), ALL, split_axis=...  24.3 us
    all_to_all x1, waiting for transfers between devices, shards(): lax.all_to_all(d_kv_blocks.reshape(planes, rows_group, KV), 'tg', split_a...  23.1 us
    all_gather x1, waiting for transfers between devices, shards(): lax.all_gather(kv_own, 'tg', axis=0, tiled=True)  19.9 us
  transfers between devices with their start and end apart: 17, of which 13 were waited for; matrix products, arithmetic and copies ran while one was open for 24% of the time, Pallas kernels for 6%

profile of v1, /device:TPU:0, one launch (start us, length us, event | category | flops | bytes accessed | tf_op | source)
XLA Modules:
  0.0 564.8 jit_solution(286849896646165126)
XLA Ops:
  12.3 38.0 %all_to_all.92 = bf16[32,48,384]{2,1,0:T(8,128)(2,1)S(1)} all-to-all(bf16[32,48,384]{2,1,0:T(8,128)(2,1)S(1)} %bitcast.111), channel_id=1, replica_groups=mesh['head'=2,'tg'=4,'hg'=4] {'head','tg','hg'}, dimensions={0} | all-to-all | bytes 2359296 | tf_op jit(solution)/shard_map/all_to_all | solution.py:283
  50.6 5.8 %all-gather.5.cloned.1.call-done = bf16[1024,1536]{1,0:T(8,128)(2,1)} async-done(((bf16[128,1536]{1,0:T(8,128)(2,1)}), bf16[1024,1536]{1,0:T(8,128)(2,1)}) %all-gather.5.cloned.1.call-update) | async-done | bytes 3145744 | tf_op jit(solution)/shard_map/all_gather | solution.py:286
  56.4 2.7 fusion
  59.2 1.8 convolution_convert_fusion.4
  70.3 19.9 %all-gather.7.cloned.1.call-done = bf16[4096,128]{1,0:T(8,128)(2,1)} async-done(((bf16[1024,128]{1,0:T(8,128)(2,1)}), bf16[4096,128]{1,0:T(8,128)(2,1)}) %all-gather.7.cloned.1.call-update) | async-done | bytes 1048592 | tf_op jit(solution)/shard_map/all_gather | solution.py:359
  90.2 17.8 %attend.1 = (bf16[1024,192]{1,0:T(8,128)(2,1)}, f32[4,3,256]{2,1,0:T(4,128)}) custom-call(s32[12]{0:T(128)} %lengths_ref.3, s32[1]{0:T(128)} %bitcast.2.meta_ref, bf16[1024,192]{1,0:T(8,128)(2,1)} %slice.124.q_ref, bf16[8,512,128]{2,1,0:T(8,128)(2,1)} %bitcast.114), custom_call_target="tpu_custom_call" | custom-call | tf_op jit(solution)/shard_map/attend/pallas_call | solution.py:181
  108.0 2.0 copy.168
  110.0 3.9 all-to-all-start.1
  115.2 6.6 %all-to-all-done.1 = bf16[8,128,192]{1,2,0:T(8,128)(2,1)S(1)} async-done(((bf16[8,128,192]{1,2,0:T(8,128)(2,1)}), bf16[8,128,192]{1,2,0:T(8,128)(2,1)S(1)}, u32[]{:S(2)}, u32[]{:S(2)}) %all-to-all-start.1) | async-done | bytes 393248 | tf_op jit(solution)/shard_map/all_to_all | solution.py:362
  121.8 36.3 %all-gather.9.cloned.1.call-done = bf16[1536,1664]{1,0:T(8,128)(2,1)} async-done(((bf16[48,1664]{1,0:T(8,128)(2,1)}), bf16[1536,1664]{1,0:T(8,128)(2,1)}) %all-gather.9.cloned.1.call-update) | async-done | bytes 5111824 | tf_op jit(solution)/shard_map/all_gather | solution.py:297
  158.1 3.2 multiply_reduce_fusion.3
  161.4 1.3 convert_reduce_fusion
  162.8 1.2 fusion.41
  166.1 1.6 convolution_convert_fusion.2
  167.7 3.3 concatenate.41
  171.0 4.5 all-to-all-start.2
  175.6 1.6 convolution_convert_fusion.1
  177.2 36.1 %all-to-all-done.2 = bf16[16,24,1664]{2,1,0:T(8,128)(2,1)} async-done(((bf16[16,24,1664]{2,1,0:T(8,128)(2,1)}), bf16[16,24,1664]{2,1,0:T(8,128)(2,1)}, u32[]{:S(2)}, u32[]{:S(2)}) %all-to-all-start.2) | async-done | bytes 1277984 | tf_op jit(solution)/shard_map/all_to_all | solution.py:328
  213.3 12.6 %all-to-all-start.4 = ((bf16[16,24,1536]{2,1,0:T(8,128)(2,1)}), bf16[16,24,1536]{2,1,0:T(8,128)(2,1)}, u32[]{:S(2)}, u32[]{:S(2)}) async-start(bf16[16,24,1536]{2,1,0:T(8,128)(2,1)} %bitcast.109), calls=%async_computation.4 | async-start | bytes 2359296 | tf_op jit(solution)/shard_map/all_to_all | solution.py:328
  226.0 43.3 %all-to-all-done.4 = bf16[16,24,1536]{2,1,0:T(8,128)(2,1)} async-done(((bf16[16,24,1536]{2,1,0:T(8,128)(2,1)}), bf16[16,24,1536]{2,1,0:T(8,128)(2,1)}, u32[]{:S(2)}, u32[]{:S(2)}) %all-to-all-start.4) | async-done | bytes 1179680 | tf_op jit(solution)/shard_map/all_to_all | solution.py:328
  269.3 1.3 add_reduce_fusion
  270.6 1.9 fusion.16
  272.8 1.4 fusion.23
  275.0 1.5 fusion.27
  276.6 5.3 multiply_reduce_fusion
  283.6 3.2 fusion.25
  286.8 3.5 convolution_add_fusion
  291.1 6.2 %concatenate.44 = f32[768,1664]{1,0:T(8,128)} concatenate(f32[768,1536]{1,0:T(8,128)} %convolution_add_fusion, f32[768,1]{1,0:T(8,128)S(1)} %copy.179, f32[768,1]{1,0:T(8,128)S(1)} %copy.180, f32[768,126]{1,0:T(8,128)} %broadcast_in_dim.117), dimensions={1} | concatenate | bytes 10223616 | tf_op jit(solution)/shard_map/concatenate | solution.py:410
  297.4 1.9 slice.199
  299.8 2.6 collective-permute-done.3
  302.4 2.0 fusion.7
  304.5 47.0 %all_to_all.93 = bf16[16,24,1664]{2,1,0:T(8,128)(2,1)S(1)} all-to-all(bf16[16,24,1664]{2,1,0:T(8,128)(2,1)S(1)} %bitcast.107), channel_id=1, replica_groups=mesh['head'=2,'tg'=4,'hg'=4] {'tg','hg'}, dimensions={0} | all-to-all | bytes 2555904 | tf_op jit(solution)/shard_map/all_to_all | solution.py:340
  353.2 1.7 fusion.29
  355.0 1.5 multiply_reduce_fusion.1
  356.8 5.0 fusion.12
  361.8 1.9 copy.183
  363.7 4.3 all-to-all-start.6
  368.0 3.4 convolution_multiply_fusion
  371.4 2.2 copy-done.12
  375.8 2.0 copy.184
  377.8 18.1 %attend_back.1 = (bf16[1024,192]{1,0:T(8,128)(2,1)}, bf16[8,512,128]{2,1,0:T(8,128)(2,1)}) custom-call(s32[12]{0:T(128)} %lengths_ref.3, s32[1]{0:T(128)} %bitcast.2.meta_ref, bf16[1024,192]{1,0:T(8,128)(2,1)} %slice.124.q_ref, bf16[1024,192]{1,0:T(8,128)(2,1)} %bitcast.122, bf16[1024,192]{1,0:T(8,128)(2,1)} %get-tuple-element.16.o_ref, ...), custom_call_target="tpu_custom_call" | custom-call | tf_op jit(solution)/shard_map/attend_back/pallas_call | solution.py:206
  395.9 3.5 all-to-all-start.7
  399.5 3.3 fusion.17
  402.8 23.1 %all-to-all-done.7 = bf16[4,1024,128]{2,1,0:T(8,128)(2,1)S(1)} async-done(((bf16[4,1024,128]{2,1,0:T(8,128)(2,1)}), bf16[4,1024,128]{2,1,0:T(8,128)(2,1)S(1)}, u32[]{:S(2)}, u32[]{:S(2)}) %all-to-all-start.7) | async-done | bytes 1048608 | tf_op jit(solution)/shard_map/all_to_all | solution.py:464
  426.9 4.3 all-to-all-start.3
  431.2 3.6 convolution_convert_fusion
  438.5 4.8 convolution_bitcast_fusion.1
  443.7 1.5 concatenate.51
  445.2 1.5 reduce_sum.186
  446.7 1.4 maximum_maximum_fusion.1
  448.1 1.2 copy.185
  449.2 8.5 %all-to-all-done.3 = bf16[16,24,1536]{2,1,0:T(8,128)(2,1)S(1)} async-done(((bf16[16,24,1536]{2,1,0:T(8,128)(2,1)}), bf16[16,24,1536]{2,1,0:T(8,128)(2,1)S(1)}, u32[]{:S(2)}, u32[]{:S(2)}) %all-to-all-start.3) | async-done | bytes 1179680 | tf_op jit(solution)/shard_map/all_to_all | solution.py:340
  457.8 4.2 all-to-all-start.8
  462.0 3.5 fusion.31
  466.5 1.7 copy.186
  468.2 2.6 maximum_maximum_fusion
  470.8 3.2 all-to-all-done.8
  474.0 4.7 all-to-all-start.9
  478.7 5.1 convolution_bitcast_fusion.2
  483.9 4.5 convolution_bitcast_fusion
  489.6 7.3 %fusion.34 = (f32[128]{0:T(128)S(1)}, f32[128]{0:T(128)S(1)}, f32[128,1536]{1,0:T(8,128)S(1)}) fusion(bf16[128,1536]{1,0:T(8,128)(2,1)S(1)} %copy-done.8, bf16[128,3072]{0,1:T(8,128)(2,1)} %bitcast.30, bf16[1536,3072]{1,0:T(8,128)(2,1)} %all-gather.11.cloned.1.call-done, f32[1536]{0:T(1024)S(1)} %copy-done.31), kind=kOutput, calls=%fused_computation.63 | convolution fusion | flops 1209138944 | bytes 11410432 | tf_op jit(solution)/shard_map/ti,di->td/dot_general | solution.py:498
  497.9 24.3 %all-to-all-done.9 = bf16[32,48,384]{2,1,0:T(8,128)(2,1)S(1)} async-done(((bf16[32,48,384]{2,1,0:T(8,128)(2,1)}), bf16[32,48,384]{2,1,0:T(8,128)(2,1)S(1)}, u32[]{:S(2)}, u32[]{:S(2)}) %all-to-all-start.9) | async-done | bytes 1179680 | tf_op jit(solution)/shard_map/all_to_all | solution.py:482
  530.9 25.3 %reduce-scatter.2.cloned.1.call-done = bf16[48,1536]{1,0:T(8,128)(2,1)} async-done(((bf16[1536,1536]{1,0:T(8,128)(2,1)}), bf16[48,1536]{1,0:T(8,128)(2,1)}) %reduce-scatter.2.cloned.1.call-update) | async-done | bytes 147472 | tf_op jit(solution)/shard_map/reduce_scatter | solution.py:457
  556.2 1.6 convert_element_type.269
  (258 shorter events, 43.1 us)
Async XLA Ops:
  7.2 269.4 %copy-start = (bf16[1,512,1536]{2,1,0:T(8,128)(2,1)S(1)}, bf16[1,512,1536]{2,1,0:T(8,128)(2,1)}, u32[]{:S(2)}) copy-start(bf16[1,512,1536]{2,1,0:T(8,128)(2,1)} %param.26) | copy-start | bytes 4718596
  7.2 49.2 %all-gather.5.cloned.1.call-start = ((), (), s32[]{:S(2)}) async-start(), calls=%async_computation.11 | async-start | bytes 3538944 | tf_op jit(solution)/shard_map/all_gather | solution.py:286
  7.9 82.3 %all-gather.7.cloned.1.call-start = ((), (), s32[]{:S(2)}) async-start(), calls=%async_computation.12 | async-start | bytes 1310720 | tf_op jit(solution)/shard_map/all_gather | solution.py:359
  9.1 3.2 copy-start.14
  50.6 8.5 %copy-start.30 = (f32[1536]{0:T(1024)}, f32[1536]{0:T(1024)S(1)}, u32[]{:S(2)}) copy-start(f32[1536]{0:T(1024)S(1)} %convert_reduce_fusion.1) | copy-start | bytes 18436
  56.4 2.8 copy-start.9
  59.2 3.7 copy-start.58
  59.2 3.8 copy-start.61
  59.2 3.9 copy-start.29
  62.0 2.8 copy-start.59
  62.0 5.4 copy-start.32
  62.8 6.6 %copy-start.28 = (bf16[1024,384]{1,0:T(8,128)(2,1)S(1)}, bf16[1024,384]{1,0:T(8,128)(2,1)}, u32[]{:S(2)}) copy-start(bf16[1024,384]{1,0:T(8,128)(2,1)} %copy-done.27) | copy-start | bytes 2359300
  62.9 95.2 %all-gather.9.cloned.1.call-start = ((), (), s32[]{:S(2)}) async-start(), calls=%async_computation.13 | async-start | bytes 5271552 | tf_op jit(solution)/shard_map/all_gather | solution.py:297
  63.9 425.7 %all-gather.11.cloned.1.call-start = ((), (), s32[]{:S(2)}) async-start(), calls=%async_computation.14 | async-start | bytes 9732096 | tf_op jit(solution)/shard_map/all_gather | solution.py:298
  90.2 67.9 %copy-start.7 = (bf16[128,1536]{1,0:T(8,128)(2,1)S(1)}, bf16[128,1536]{1,0:T(8,128)(2,1)}, u32[]{:S(2)}) copy-start(bf16[128,1536]{1,0:T(8,128)(2,1)} %param.14) | copy-start | bytes 1179652
  110.0 11.8 %all-to-all-start.1 = ((bf16[8,128,192]{1,2,0:T(8,128)(2,1)}), bf16[8,128,192]{1,2,0:T(8,128)(2,1)S(1)}, u32[]{:S(2)}, u32[]{:S(2)}) async-start(bf16[8,128,192]{1,2,0:T(8,128)(2,1)} %copy.168), calls=%async_computation.1 | async-start | bytes 786432 | tf_op jit(solution)/shard_map/all_to_all | solution.py:362
  121.8 39.5 %copy-start.10 = (bf16[8,128,192]{1,2,0:T(8,128)(2,1)}, bf16[8,128,192]{1,2,0:T(8,128)(2,1)S(1)}, u32[]{:S(2)}) copy-start(bf16[8,128,192]{1,2,0:T(8,128)(2,1)S(1)} %all-to-all-done.1) | copy-start | bytes 1179652
  161.3 4.1 copy-start.43
  161.3 4.8 copy-start.33
  161.3 4.7 copy-start.37
  171.0 4.5 copy-start.16
  171.0 4.6 copy-start.34
  171.0 4.6 copy-start.38
  171.0 42.3 %all-to-all-start.2 = ((bf16[16,24,1664]{2,1,0:T(8,128)(2,1)}), bf16[16,24,1664]{2,1,0:T(8,128)(2,1)}, u32[]{:S(2)}, u32[]{:S(2)}) async-start(bf16[16,24,1664]{2,1,0:T(8,128)(2,1)} %concatenate.41), calls=%async_computation.2 | async-start | bytes 2555904 | tf_op jit(solution)/shard_map/all_to_all | solution.py:328
  213.3 56.0 %all-to-all-start.4 = ((bf16[16,24,1536]{2,1,0:T(8,128)(2,1)}), bf16[16,24,1536]{2,1,0:T(8,128)(2,1)}, u32[]{:S(2)}, u32[]{:S(2)}) async-start(bf16[16,24,1536]{2,1,0:T(8,128)(2,1)} %bitcast.109), calls=%async_computation.4 | async-start | bytes 2359296 | tf_op jit(solution)/shard_map/all_to_all | solution.py:328
  225.9 43.4 %collective-permute-start = (bf16[384,1664]{1,0:T(8,128)(2,1)}, bf16[384,1664]{1,0:T(8,128)(2,1)}, u32[]{:S(2)}, u32[]{:S(2)}) collective-permute-start(bf16[384,1664]{1,0:T(8,128)(2,1)} %bitcast.14), channel_id=1, source_target_pairs={{0,16},{16,0},{1,17},{17,1},{2,18},{18,2},{3,19},{19,3},{4,20},{20... | collective-permute-start | bytes 3833864 | tf_op jit(solution)/shard_map/ppermute | solution.py:335
  269.3 7.2 %collective-permute-start.2 = (bf16[384,1536]{1,0:T(8,128)(2,1)}, bf16[384,1536]{1,0:T(8,128)(2,1)S(1)}, u32[]{:S(2)}, u32[]{:S(2)}) collective-permute-start(bf16[384,1536]{1,0:T(8,128)(2,1)} %bitcast.21), channel_id=1, source_target_pairs={{0,16},{16,0},{1,17},{17,1},{2,18},{18,2},{3,19},{19,3},{4,20},{20... | collective-permute-start | bytes 3538952 | tf_op jit(solution)/shard_map/ppermute | solution.py:335
  270.6 5.9 %copy-start.52 = (f32[768]{0:T(1024)}, f32[768]{0:T(1024)S(1)}, u32[]{:S(2)}) copy-start(f32[768]{0:T(1024)S(1)} %add_reduce_fusion) | copy-start | bytes 9220
  272.8 2.3 copy-start.62
  276.5 5.4 copy-start.69
  276.5 5.4 copy-start.63
  283.5 3.3 copy-start.19
  283.6 3.3 copy-start.24
  299.2 3.2 collective-permute-start.3
  304.5 48.3 %copy-start.44 = (s32[256]{0:T(256)S(1)}, s32[256]{0:T(256)}, u32[]{:S(2)}) copy-start(s32[256]{0:T(256)} %and_select_fusion) | copy-start | bytes 3076
  304.5 48.7 %copy-start.42 = (f32[128]{0:T(128)S(1)}, f32[128]{0:T(128)}, u32[]{:S(2)}) copy-start(f32[128]{0:T(128)} %copy-done.41) | copy-start | bytes 1540
  304.5 48.6 %copy-start.46 = (f32[128]{0:T(128)S(1)}, f32[128]{0:T(128)}, u32[]{:S(2)}) copy-start(f32[128]{0:T(128)} %copy-done.45) | copy-start | bytes 1540
  304.5 48.7 %copy-start.35 = (s32[128]{0:T(128)S(1)}, s32[128]{0:T(128)}, u32[]{:S(2)}) copy-start(s32[128]{0:T(128)} %get-tuple-element.72) | copy-start | bytes 1540
  304.5 48.7 %copy-start.39 = (s32[128]{0:T(128)S(1)}, s32[128]{0:T(128)}, u32[]{:S(2)}) copy-start(s32[128]{0:T(128)} %get-tuple-element.73) | copy-start | bytes 1540
  351.5 3.4 copy-start.48
  356.8 74.4 %copy-start.2 = (f32[128,1536]{1,0:T(8,128)}, f32[128,1536]{1,0:T(8,128)S(1)}, u32[]{:S(2)}) copy-start(f32[128,1536]{1,0:T(8,128)S(1)} %multiply_subtract_fusion) | copy-start | bytes 2359300
  361.8 6.2 %copy-start.53 = (f32[768]{0:T(1024)S(1)}, f32[768]{0:T(1024)}, u32[]{:S(2)}) copy-start(f32[768]{0:T(1024)} %copy-done.52) | copy-start | bytes 9220
  363.7 12.1 %all-to-all-start.6 = ((bf16[128,8,192]{0,2,1:T(8,128)(2,1)}), bf16[128,8,192]{0,2,1:T(8,128)(2,1)}, u32[]{:S(2)}, u32[]{:S(2)}) async-start(bf16[128,8,192]{0,2,1:T(8,128)(2,1)} %bitcast.125), calls=%async_computation.6 | async-start | bytes 786432 | tf_op jit(solution)/shard_map/all_to_all | solution.py:455
  374.8 24.7 %collective-permute-start.1 = (bf16[384,1536]{1,0:T(8,128)(2,1)}, bf16[384,1536]{1,0:T(8,128)(2,1)}, u32[]{:S(2)}, u32[]{:S(2)}) collective-permute-start(bf16[384,1536]{1,0:T(8,128)(2,1)} %slice.200), channel_id=1, source_target_pairs={{0,16},{16,0},{1,17},{17,1},{2,18},{18,2},{3,19},{19,3},{4,20},{20... | collective-permute-start | bytes 3538952 | tf_op jit(solution)/shard_map/ppermute | solution.py:338
  395.9 30.0 %all-to-all-start.7 = ((bf16[4,1024,128]{2,1,0:T(8,128)(2,1)}), bf16[4,1024,128]{2,1,0:T(8,128)(2,1)S(1)}, u32[]{:S(2)}, u32[]{:S(2)}) async-start(bf16[4,1024,128]{2,1,0:T(8,128)(2,1)} %bitcast.129), calls=%async_computation.7 | async-start | bytes 2097152 | tf_op jit(solution)/shard_map/all_to_all | solution.py:464
  402.8 28.4 %copy-start.11 = (bf16[8,128,192]{1,2,0:T(8,128)(2,1)S(1)}, bf16[8,128,192]{1,2,0:T(8,128)(2,1)}, u32[]{:S(2)}) copy-start(bf16[8,128,192]{1,2,0:T(8,128)(2,1)} %copy-done.10) | copy-start | bytes 1179652
  426.9 30.9 %all-to-all-start.3 = ((bf16[16,24,1536]{2,1,0:T(8,128)(2,1)}), bf16[16,24,1536]{2,1,0:T(8,128)(2,1)S(1)}, u32[]{:S(2)}, u32[]{:S(2)}) async-start(bf16[16,24,1536]{2,1,0:T(8,128)(2,1)} %bitcast.112), calls=%async_computation.3 | async-start | bytes 2359296 | tf_op jit(solution)/shard_map/all_to_all | solution.py:340
  431.2 125.0 %reduce-scatter.2.cloned.1.call-start = ((), (), s32[]{:S(2)}) async-start(), calls=%async_computation.15 | async-start | bytes 4866048 | tf_op jit(solution)/shard_map/reduce_scatter | solution.py:457
  434.8 2.3 copy-start.21
  434.8 3.7 copy-start.25
  448.0 14.0 %copy-start.31 = (f32[1536]{0:T(1024)S(1)}, f32[1536]{0:T(1024)}, u32[]{:S(2)}) copy-start(f32[1536]{0:T(1024)} %copy-done.30) | copy-start | bytes 18436
  448.0 14.0 %copy-start.57 = (f32[1024]{0:T(1024)S(1)}, f32[1024]{0:T(1024)}, u32[]{:S(2)}) copy-start(f32[1024]{0:T(1024)} %copy-done.56) | copy-start | bytes 12292
  457.8 16.2 %all-to-all-start.8 = ((bf16[8,128,384]{1,2,0:T(8,128)(2,1)}), bf16[8,128,384]{1,2,0:T(8,128)(2,1)}, u32[]{:S(2)}, u32[]{:S(2)}) async-start(bf16[8,128,384]{1,2,0:T(8,128)(2,1)} %copy.185), calls=%async_computation.8 | async-start | bytes 1572864 | tf_op jit(solution)/shard_map/all_to_all | solution.py:471
  474.0 48.2 %all-to-all-start.9 = ((bf16[32,48,384]{2,1,0:T(8,128)(2,1)}), bf16[32,48,384]{2,1,0:T(8,128)(2,1)S(1)}, u32[]{:S(2)}, u32[]{:S(2)}) async-start(bf16[32,48,384]{2,1,0:T(8,128)(2,1)} %maximum_maximum_fusion), calls=%async_computation.9 | async-start | bytes 2359296 | tf_op jit(solution)/shard_map/all_to_all | solution.py:482
  478.7 5.1 copy-start.54
  478.7 5.1 copy-start.64
  478.7 5.1 copy-start.68
  478.7 5.1 copy-start.70
  483.9 4.5 copy-start.36
  483.9 4.5 copy-start.40
  483.9 4.5 copy-start.51
  489.6 7.3 %copy-start.3 = (f32[128,1536]{1,0:T(8,128)S(1)}, f32[128,1536]{1,0:T(8,128)}, u32[]{:S(2)}) copy-start(f32[128,1536]{1,0:T(8,128)} %copy-done.2) | copy-start | bytes 2359300
  527.3 30.5 %copy-start.1 = (bf16[1,512,1536]{2,1,0:T(8,128)(2,1)S(1)}, bf16[1,512,1536]{2,1,0:T(8,128)(2,1)}, u32[]{:S(2)}) copy-start(bf16[1,512,1536]{2,1,0:T(8,128)(2,1)} %param.26) | copy-start | bytes 4718596
  527.5 2.8 copy-start.60
  (24 other events, 34.8 us)
Sparse Core Ops, SparseCore 0:
  9.9 46.4 all-gather.4
  63.0 27.1 all-gather.6
  93.7 64.3 all-gather.8
  161.4 120.1 all-gather.10
  437.2 119.0 reduce-scatter.1

commit v2 on v1

--- a/solution.py
+++ b/solution.py
@@ -284,18 +284,16 @@
         to_send.reshape(devices, rows_dev, slab), ALL, split_axis=0, concat_axis=0, tiled=True
     ).reshape(D, slab)
     x_group = lax.all_gather(tokens, PLANE, axis=0, tiled=True)
-    extra = pad_up(experts + 1)
     out_shard = jnp.concatenate(
         [
             w_out,
             w_router,
             gain_moe[:, None],
-            jnp.zeros((rows_dev, extra - experts - 1), BF16),
+            jnp.zeros((rows_dev, pad_up(experts + 1) - experts - 1), BF16),
         ],
         axis=1,
     )
     full_out = lax.all_gather(out_shard, ALL, axis=0, tiled=True)
-    full_in = lax.all_gather(by_group.reshape(rows_dev, in_group * slab), ALL, axis=0, tiled=True)
 
     seq_ends = jnp.cumsum(lengths)
     own_pos = (lax.axis_index("head") * blk_count + blk_index) * tok_dev + jnp.arange(
@@ -303,52 +301,52 @@
     )
     valid_bool = own_pos < seq_ends[-2]
     valid_float = valid_bool.astype(F32)[:, None]
+    expert_range = jnp.arange(experts, dtype=jnp.int32)
     pair_experts = expert_ids.reshape(-1)
     live_pairs = jnp.repeat(valid_bool, 2)
     onehot = (
-        (pair_experts[:, None] == jnp.arange(experts, dtype=jnp.int32)[None, :])
-        & live_pairs[:, None]
+        (pair_experts[:, None] == expert_range[None, :]) & live_pairs[:, None]
     ).astype(jnp.int32)
     earlier = jnp.cumsum(onehot, axis=0) - onehot
     slot_index = jnp.sum(earlier * onehot, axis=1)
     kept_pairs = live_pairs & (slot_index < capacity)
     flat_index = jnp.where(kept_pairs, pair_experts * capacity + slot_index, -1)
     slot_ids = jnp.arange(slots, dtype=jnp.int32)
-    slot_bool = flat_index[None, :] == slot_ids[:, None]
     token_index = flat_index.reshape(tok_dev, 2)
     token_table = (
         (token_index[:, 0][:, None] == slot_ids[None, :])
         | (token_index[:, 1][:, None] == slot_ids[None, :])
     ).astype(BF16)
-    pick_table = (
-        expert_ids[:, :, None] == jnp.arange(experts, dtype=jnp.int32)[None, None, :]
-    ).astype(F32)
-
-    def to_experts(rows):
-        sent = lax.all_to_all(
+    picked = (expert_ids[:, 0][:, None] == expert_range[None, :]) | (
+        expert_ids[:, 1][:, None] == expert_range[None, :]
+    )
+    side = pad_up(2 * experts)
+    side_zeros = jnp.zeros((tok_dev, side - 2 * experts), BF16)
+    side_range = jnp.arange(side, dtype=jnp.int32)
+    mine = side_range % experts == blk_index
+    mine_high = mine & (side_range < experts)
+    mine_low = mine & (side_range >= experts) & (side_range < 2 * experts)
+
+    def exchange(rows):
+        return lax.all_to_all(
             rows.reshape(experts, capacity, rows.shape[1]),
             BLK,
             split_axis=0,
             concat_axis=0,
             tiled=True,
         ).reshape(slots, rows.shape[1])
+
+    def with_partner(sent):
         return jnp.concatenate([sent, lax.ppermute(sent, "head", partner)], axis=0)
 
-    def to_tokens(partial):
+    def pair_sum(partial):
         theirs = lax.ppermute(partial[slots:].astype(BF16), "head", partner)
-        summed = (partial[:slots] + theirs.astype(F32)).astype(BF16)
-        return lax.all_to_all(
-            summed.reshape(experts, capacity, summed.shape[1]),
-            BLK,
-            split_axis=0,
-            concat_axis=0,
-            tiled=True,
-        ).reshape(slots, summed.shape[1])
+        return (partial[:slots] + theirs.astype(F32)).astype(BF16)
 
     def pick_rows(values):
         return lax.dot_general(
             token_table, values, (((0,), (0,)), ((), ())), preferred_element_type=F32
-        )
+        ).astype(BF16)
 
     x_float = x_group.astype(F32)
     gain_one = own_slab[:, QKV].astype(F32)[None, :]
@@ -356,12 +354,22 @@
     qkv = jnp.dot(normed_one, own_slab, preferred_element_type=F32).astype(BF16)
     query = qkv[:, :QW]
     kv_own = qkv[:, QW:QKV]
-    kv_blocks = lax.all_gather(kv_own, "tg", axis=0, tiled=True).reshape(planes * 2, run, KV)
+    with jax.named_scope("kv_send"):
+        kv_blocks = lax.all_to_all(
+            jnp.broadcast_to(kv_own[None], (planes, rows_group, KV)),
+            "tg",
+            split_axis=0,
+            concat_axis=0,
+            tiled=True,
+        ).reshape(planes * 2, run, KV)
+    d_send = pick_rows(cotangent)
+    d_send, kv_blocks = lax.optimization_barrier((d_send, kv_blocks))
+    with jax.named_scope("d_send"):
+        d_sent = exchange(d_send)
     meta = plane.astype(jnp.int32).reshape(1)
-    attn_rows, lse = attend(lengths, meta, query, kv_blocks, planes)
+    with jax.named_scope("attention"):
+        attn_rows, lse = attend(lengths, meta, query, kv_blocks, planes)
     attn_tokens = lax.all_to_all(attn_rows, PLANE, split_axis=0, concat_axis=1, tiled=True)
-
-    d_rows = to_experts(pick_rows(cotangent).astype(BF16))
 
     own_x = tokens.astype(F32)
     hidden_one = own_x + jnp.dot(attn_tokens, full_out[:, :D], preferred_element_type=F32)
@@ -370,26 +378,22 @@
     router = full_out[:, D : D + experts]
     normed_two = (hidden_one * scale_two * gain_two).astype(BF16)
     logits = jnp.dot(normed_two, router, preferred_element_type=F32)
-    mix = jax.nn.softmax(jnp.sum(pick_table * logits[:, None, :], axis=2), axis=1)
-    slot_mix = jnp.sum(jnp.where(slot_bool, mix.reshape(1, -1), 0.0), axis=1, keepdims=True)
-    mix_high, mix_low = split_float(slot_mix)
-    moe_rows = to_experts(
-        jnp.concatenate(
-            [
-                pick_rows(normed_two).astype(BF16),
-                mix_high,
-                mix_low,
-                jnp.zeros((slots, LANE - 2), BF16),
-            ],
-            axis=1,
-        )
-    )
+    mix = jax.nn.softmax(jnp.where(picked, logits, NEG), axis=1)
+    mix_high, mix_low = split_float(mix)
+    moe_send = pick_rows(jnp.concatenate([normed_two, mix_high, mix_low, side_zeros], axis=1))
+    with jax.named_scope("moe_send"):
+        moe_sent = exchange(moe_send)
+    moe_rows = with_partner(moe_sent)
+    with jax.named_scope("d_swap"):
+        d_rows = with_partner(d_sent)
 
     gate_mat = w_gate[0]
     up_mat = w_up[0]
     down_mat = w_down[0]
     rows = moe_rows[:, :D]
-    row_mix = moe_rows[:, D : D + 1].astype(F32) + moe_rows[:, D + 1 : D + 2].astype(F32)
+    row_mix = jnp.sum(
+        jnp.where(mine_high | mine_low, moe_rows[:, D:].astype(F32), 0.0), axis=1, keepdims=True
+    )
     gate_pre = jnp.dot(rows, gate_mat, preferred_element_type=F32)
     up_pre = jnp.dot(rows, up_mat, preferred_element_type=F32)
     sigmoid_gate = jax.nn.sigmoid(gate_pre)
@@ -406,35 +410,34 @@
         "rf,df->rd", d_up, up_mat, preferred_element_type=F32
     )
     mix_part_high, mix_part_low = split_float(d_mix_part)
-    d_back = to_tokens(
-        jnp.concatenate(
-            [
-                d_in,
-                mix_part_high.astype(F32),
-                mix_part_low.astype(F32),
-                jnp.zeros((2 * slots, LANE - 2), F32),
-            ],
-            axis=1,
-        )
-    )
-    y_back = to_tokens(jnp.dot(inner_act, down_mat, preferred_element_type=F32) * row_mix)
-    output = (
-        valid_float * (hidden_one + jnp.dot(token_table, y_back, preferred_element_type=F32))
-    ).astype(BF16)
+    side_back = jnp.where(
+        mine_high, mix_part_high, jnp.where(mine_low, mix_part_low, jnp.zeros((), BF16))
+    )
+    d_sum = pair_sum(d_in)
+    side_sum = side_back[:slots].astype(F32) + lax.ppermute(
+        side_back[slots:], "head", partner
+    ).astype(F32)
+    d_mix_high, d_mix_low = split_float(jnp.sum(side_sum, axis=1, keepdims=True))
+    side_own = jnp.where(
+        mine_high, d_mix_high, jnp.where(mine_low, d_mix_low, jnp.zeros((), BF16))
+    )
+    with jax.named_scope("moe_back"):
+        d_back = exchange(jnp.concatenate([d_sum, side_own], axis=1))
+    y_send = pair_sum(jnp.dot(inner_act, down_mat, preferred_element_type=F32) * row_mix)
     d_y = (d_rows.astype(F32) * row_mix).astype(BF16)
-    grad_gate = jnp.einsum("rd,rf->df", rows, d_gate, preferred_element_type=F32)[None]
-    grad_up = jnp.einsum("rd,rf->df", rows, d_up, preferred_element_type=F32)[None]
-    grad_down = jnp.einsum("rf,rd->fd", inner_act, d_y, preferred_element_type=F32)[None]
+    with jax.named_scope("expert_grads"):
+        grad_gate = jnp.einsum("rd,rf->df", rows, d_gate, preferred_element_type=F32)[None]
+        grad_up = jnp.einsum("rd,rf->df", rows, d_up, preferred_element_type=F32)[None]
+        grad_down = jnp.einsum("rf,rd->fd", inner_act, d_y, preferred_element_type=F32)[None]
 
     d_out = cotangent.astype(F32) * valid_float
-    slot_d_mix = d_back[:, D : D + 1].astype(F32) + d_back[:, D + 1 : D + 2].astype(F32)
-    d_mix = jnp.sum(jnp.where(slot_bool, slot_d_mix, 0.0), axis=0).reshape(tok_dev, 2)
-    d_chosen = mix * (d_mix - jnp.sum(mix * d_mix, axis=1, keepdims=True))
-    d_logits = jnp.sum(pick_table * d_chosen[:, :, None], axis=1).astype(BF16)
+    d_token = jnp.dot(token_table, d_back, preferred_element_type=F32)
+    d_mix = d_token[:, D : D + experts] + d_token[:, D + experts : D + 2 * experts]
+    d_logits = (mix * (d_mix - jnp.sum(mix * d_mix, axis=1, keepdims=True))).astype(BF16)
     grad_router_part = jnp.einsum("td,te->de", normed_two, d_logits, preferred_element_type=F32)
-    d_normed_two = jnp.dot(
-        token_table, d_back[:, :D], preferred_element_type=F32
-    ) + jnp.einsum("te,de->td", d_logits, router, preferred_element_type=F32)
+    d_normed_two = d_token[:, :D] + jnp.einsum(
+        "te,de->td", d_logits, router, preferred_element_type=F32
+    )
     gain_moe_part = jnp.sum(d_normed_two * hidden_one * scale_two, axis=0)
     along_two = gain_two * d_normed_two
     d_hidden = (
@@ -453,14 +456,25 @@
         BF16
     )
     d_attn_rows = lax.all_to_all(d_attn, PLANE, split_axis=1, concat_axis=0, tiled=True)
-    grad_out_part = jnp.einsum("ti,td->id", attn_tokens, d_proj, preferred_element_type=F32)
-    grad_out = lax.psum_scatter(
-        grad_out_part.astype(BF16), ALL, scatter_dimension=0, tiled=True
-    ).astype(F32)
-
-    d_query, d_kv_blocks = attend_back(
-        lengths, meta, query, d_attn_rows, attn_rows, lse, kv_blocks, planes
-    )
+    grad_out_part = jnp.einsum(
+        "ti,td->id", attn_tokens, d_proj, preferred_element_type=F32
+    ).astype(BF16)
+    grad_out_part, d_attn_rows = lax.optimization_barrier((grad_out_part, d_attn_rows))
+    with jax.named_scope("grad_out"):
+        grad_out = lax.psum_scatter(
+            grad_out_part, ALL, scatter_dimension=0, tiled=True
+        ).astype(F32)
+    y_send, d_attn_rows = lax.optimization_barrier((y_send, d_attn_rows))
+    with jax.named_scope("y_send"):
+        y_back = exchange(y_send)
+    output = (
+        valid_float * (hidden_one + jnp.dot(token_table, y_back, preferred_element_type=F32))
+    ).astype(BF16)
+
+    with jax.named_scope("attention_back"):
+        d_query, d_kv_blocks = attend_back(
+            lengths, meta, query, d_attn_rows, attn_rows, lse, kv_blocks, planes
+        )
     d_kv_parts = lax.all_to_all(
         d_kv_blocks.reshape(planes, rows_group, KV), "tg", split_axis=0, concat_axis=0, tiled=True
     )
@@ -468,7 +482,6 @@
     d_qkv = jnp.concatenate(
         [d_query, d_kv, jnp.zeros((rows_group, slab - QKV), BF16)], axis=1
     )
-    d_tokens = lax.all_to_all(d_qkv, PLANE, split_axis=0, concat_axis=1, tiled=True)
     grad_in = jnp.einsum("td,ti->di", normed_one, d_qkv, preferred_element_type=F32)
     grad_in = jnp.concatenate(
         [
@@ -479,9 +492,16 @@
         ],
         axis=1,
     ).astype(BF16)
-    grad_parts = lax.all_to_all(
-        grad_in.reshape(devices, rows_dev, slab), ALL, split_axis=0, concat_axis=0, tiled=True
-    ).astype(F32)
+    with jax.named_scope("grad_send"):
+        grad_parts = lax.all_to_all(
+            grad_in.reshape(devices, rows_dev, slab), ALL, split_axis=0, concat_axis=0, tiled=True
+        )
+    d_normed_part = jnp.einsum("ti,di->td", d_qkv, own_slab, preferred_element_type=F32)
+    with jax.named_scope("d_normed"):
+        d_normed_one = lax.psum_scatter(
+            d_normed_part.astype(BF16), PLANE, scatter_dimension=0, tiled=True
+        ).astype(F32)
+    grad_parts = grad_parts.astype(F32)
     grad_small = jnp.sum(grad_parts[:, :, QKV:], axis=0)
     grad_router = grad_small[:, :experts]
     grad_gain_moe = grad_small[:, experts]
@@ -495,7 +515,6 @@
     grad_gain_attn = (
         jnp.sum(grad_qkv * by_group[:, :, :QKV].astype(F32), axis=(1, 2)) / gain_attn.astype(F32)
     )
-    d_normed_one = jnp.einsum("ti,di->td", d_tokens, full_in, preferred_element_type=F32)
     scale_one = rms_scale(own_x)
     along_one = gain_one * d_normed_one
     input_grad = (

time: 574 us -> 484 us (0.84)
  waiting for transfers between devices: 236 us -> 118 us
  blocking collectives: 85 us -> 163 us
  starting transfers between devices: 43.4 us -> 28.7 us
  local copies, waits for them, and re-layouts: 53.5 us -> 39.5 us
  matrix products: 66.2 us -> 55.9 us
    all_to_all x1 -> x3, blocking collectives: 47 us -> 125 us  [the longest x2 75.6 us: exchange(): lax.all_to_all(rows.reshape(experts, capacity, rows.shape[1]), BLK, split...]
    all_to_all x5 -> x3, waiting for transfers between devices: 114 us -> 57.2 us  [the longest x2 35.1 us: exchange(): lax.all_to_all(rows.reshape(experts, capacity, rows.shape[1]), BLK, split...]
    all_gather x1, waiting for transfers between devices: 36.3 us -> 8.02 us  [shards(): full_out = lax.all_gather(out_shard, ALL, axis=0, tiled=True)]
    all_gather x2 -> x0, waiting for transfers between devices: 19.9 us -> none  [the longest x1 19.9 us: shards(): lax.all_gather(kv_own, 'tg', axis=0, tiled=True)]
    all_to_all x5 -> x3, starting transfers between devices: 29.1 us -> 12.6 us  [the longest x2 8.26 us: exchange(): lax.all_to_all(rows.reshape(experts, capacity, rows.shape[1]), BLK, split...]
    reduce_scatter x1 -> x2, waiting for transfers between devices: 25.3 us -> 13.6 us  [the longest x1 13.6 us: shards(): lax.psum_scatter(d_normed_part.astype(BF16), PLANE, scatter_dimension=0,...]
    all_to_all x1, waiting for transfers between devices: 24.3 us -> 15.2 us  [shards(): lax.all_to_all(grad_in.reshape(devices, rows_dev, slab), ALL, split_axis=...]
    concatenate x2 -> x1, local copies, waits for them, and re-layouts: 9.49 us -> 0.86 us  [shards(): jnp.concatenate([normed_two, mix_high, mix_low, side_zeros], axis=1)]
  transfers between devices with their start and end apart: 17 -> 15, of which waited for: 13 -> 11; matrix products, arithmetic and copies ran while one was open for 24% -> 18% of each run, Pallas kernels for 6% -> 6%
where the time goes in v2:
time: 484 us; the launch traced here: 477 us
  blocking collectives  163 us (34%)
  waiting for transfers between devices  118 us (24%)
  matrix products  55.9 us (12%)
  local copies, waits for them, and re-layouts  39.5 us (8%)
  Pallas kernels  30.6 us (6%)
  starting transfers between devices  28.7 us (6%)
  other arithmetic  26.6 us (5%)
  between operations  15.2 us (3%)
    all_to_all x2, blocking collectives, exchange(): lax.all_to_all(rows.reshape(experts, capacity, rows.shape[1]), BLK, split...  75.6 us
    all_to_all x1, blocking collectives, shards(): lax.all_to_all(d_kv_blocks.reshape(planes, rows_group, KV), 'tg', split_a...  49 us
    all_to_all x1, blocking collectives, shards(): lax.all_to_all(to_send.reshape(devices, rows_dev, slab), ALL, split_axis=...  38 us
    all_to_all x2, waiting for transfers between devices, exchange(): lax.all_to_all(rows.reshape(experts, capacity, rows.shape[1]), BLK, split...  35.1 us
    all_to_all x1, waiting for transfers between devices, shards(): lax.all_to_all(jnp.broadcast_to(kv_own[None], (planes, rows_group, KV)),...  22.1 us
    pallas_call x1, Pallas kernels, attend_back(): pl.pallas_call(functools.partial(attend_back_kernel, segments=lengths.sha...  15.6 us
    all_to_all x1, waiting for transfers between devices, shards(): lax.all_to_all(grad_in.reshape(devices, rows_dev, slab), ALL, split_axis=...  15.2 us
    pallas_call x1, Pallas kernels, attend(): pl.pallas_call(functools.partial(attend_kernel, segments=lengths.shape[0]...  15 us
  transfers between devices with their start and end apart: 15, of which 11 were waited for; matrix products, arithmetic and copies ran while one was open for 18% of the time, Pallas kernels for 6%

profile of v2, /device:TPU:0, one launch (start us, length us, event | category | flops | bytes accessed | tf_op | source)
XLA Modules:
  0.0 477.0 jit_solution(7468817603238608419)
XLA Ops:
  9.5 1.7 concatenate.36
  11.2 1.1 reshape.242
  14.9 38.0 %all_to_all.78 = bf16[32,48,384]{2,1,0:T(8,128)(2,1)S(1)} all-to-all(bf16[32,48,384]{2,1,0:T(8,128)(2,1)S(1)} %bitcast.112), channel_id=1, replica_groups=mesh['head'=2,'tg'=4,'hg'=4] {'head','tg','hg'}, dimensions={0} | all-to-all | bytes 2359296 | tf_op jit(solution)/shard_map/all_to_all | solution.py:283
  53.2 3.2 all-gather.3.cloned.1.call-done
  56.5 2.7 fusion
  59.3 1.8 convolution_convert_fusion.5
  63.3 4.3 all-to-all-start.1
  70.5 1.2 fusion.67
  72.6 1.6 convolution_convert_fusion.3
  75.1 22.1 %all-to-all-done.1 = bf16[4,1024,128]{2,1,0:T(8,128)(2,1)S(1)} async-done(((bf16[4,1024,128]{2,1,0:T(8,128)(2,1)}), bf16[4,1024,128]{2,1,0:T(8,128)(2,1)S(1)}, u32[]{:S(2)}, u32[]{:S(2)}) %all-to-all-start.1) | async-done | bytes 1048608 | tf_op jit(solution)/shard_map/kv_send/all_to_all | solution.py:358
  98.1 15.0 %attend.1 = (bf16[1024,192]{1,0:T(8,128)(2,1)}, f32[4,3,256]{2,1,0:T(4,128)}) custom-call(s32[12]{0:T(128)} %lengths_ref.3, s32[1]{0:T(128)} %bitcast.2.meta_ref, bf16[1024,192]{1,0:T(8,128)(2,1)} %slice.136.q_ref, bf16[8,512,128]{2,1,0:T(8,128)(2,1)} %bitcast.102), custom_call_target="tpu_custom_call" | custom-call | tf_op jit(solution)/shard_map/attention/attend/pallas_call | solution.py:181
  113.1 2.0 copy.116
  115.1 3.5 all-to-all-start.2
  118.6 12.3 %all-to-all-done.2 = bf16[8,128,192]{1,2,0:T(8,128)(2,1)S(1)} async-done(((bf16[8,128,192]{1,2,0:T(8,128)(2,1)}), bf16[8,128,192]{1,2,0:T(8,128)(2,1)S(1)}, u32[]{:S(2)}, u32[]{:S(2)}) %all-to-all-start.2) | async-done | bytes 393248 | tf_op jit(solution)/shard_map/all_to_all | solution.py:372
  130.8 8.0 %all-gather.5.cloned.1.call-done = bf16[1536,1664]{1,0:T(8,128)(2,1)} async-done(((bf16[48,1664]{1,0:T(8,128)(2,1)}), bf16[1536,1664]{1,0:T(8,128)(2,1)}) %all-gather.5.cloned.1.call-update) | async-done | bytes 5111824 | tf_op jit(solution)/shard_map/all_gather | solution.py:296
  138.9 3.2 multiply_reduce_fusion.3
  142.1 1.3 convert_reduce_fusion
  143.6 1.5 fusion.69
  146.3 1.6 convolution_convert_fusion.2
  147.9 37.2 %all_to_all.79 = bf16[16,24,1664]{2,1,0:T(8,128)(2,1)} all-to-all(bf16[16,24,1664]{2,1,0:T(8,128)(2,1)S(1)} %bitcast.108), channel_id=1, replica_groups=mesh['head'=2,'tg'=4,'hg'=4] {'tg','hg'}, dimensions={0} | all-to-all | bytes 2555904 | tf_op jit(solution)/shard_map/moe_send/all_to_all | solution.py:331
  185.1 4.6 all-to-all-start.4
  189.8 25.7 %all-to-all-done.4 = bf16[16,24,1536]{2,1,0:T(8,128)(2,1)} async-done(((bf16[16,24,1536]{2,1,0:T(8,128)(2,1)}), bf16[16,24,1536]{2,1,0:T(8,128)(2,1)}, u32[]{:S(2)}, u32[]{:S(2)}) %all-to-all-start.4) | async-done | bytes 1179680 | tf_op jit(solution)/shard_map/d_send/all_to_all | solution.py:331
  215.4 1.2 select_reduce_fusion
  216.8 1.5 fusion.15
  218.6 1.5 fusion.23
  220.9 1.5 fusion.27
  222.4 4.2 multiply_convert_fusion.3
  226.6 1.4 fusion.25
  228.1 1.4 convolution_add_fusion
  230.6 2.1 collective-permute-done.4
  233.6 38.4 %all_to_all.80 = bf16[16,24,1664]{2,1,0:T(8,128)(2,1)S(1)} all-to-all(bf16[16,24,1664]{2,1,0:T(8,128)(2,1)S(1)} %bitcast.107), channel_id=1, replica_groups=mesh['head'=2,'tg'=4,'hg'=4] {'tg','hg'}, dimensions={0} | all-to-all | bytes 2555904 | tf_op jit(solution)/shard_map/moe_back/all_to_all | solution.py:331
  274.8 2.4 fusion.11
  277.2 1.9 copy.120
  279.1 4.1 all-to-all-start.6
  283.5 4.5 convolution_convert_fusion
  288.0 3.0 all-to-all-done.6
  291.0 2.0 copy.121
  293.7 3.4 convolution_multiply_fusion
  297.7 2.7 collective-permute-done.1
  300.3 1.4 fusion.17
  301.7 15.6 %attend_back.1 = (bf16[1024,192]{1,0:T(8,128)(2,1)}, bf16[8,512,128]{2,1,0:T(8,128)(2,1)}) custom-call(s32[12]{0:T(128)} %lengths_ref.3, s32[1]{0:T(128)} %bitcast.2.meta_ref, bf16[1024,192]{1,0:T(8,128)(2,1)} %slice.136.q_ref, bf16[1024,192]{1,0:T(8,128)(2,1)} %bitcast.117, bf16[1024,192]{1,0:T(8,128)(2,1)} %get-tuple-element.23.o_ref, ...), custom_call_target="tpu_custom_call" | custom-call | tf_op jit(solution)/shard_map/attention_back/attend_back/pallas_call | solution.py:206
  317.3 49.0 %all_to_all.81 = bf16[4,1024,128]{2,1,0:T(8,128)(2,1)} all-to-all(bf16[4,1024,128]{2,1,0:T(8,128)(2,1)} %bitcast.125), channel_id=1, replica_groups=mesh['head'=2,'tg'=4,'hg'=4] {'tg'}, dimensions={0} | all-to-all | bytes 2097152 | tf_op jit(solution)/shard_map/all_to_all | solution.py:478
  366.3 3.7 all-to-all-start.7
  370.1 1.5 reduce_sum.160
  371.6 5.1 %convolution_convert_fusion.1 = bf16[1024,1536]{1,0:T(8,128)(2,1)} fusion(bf16[1536,384]{1,0:T(8,128)(2,1)} %bitcast.120, bf16[1024,128]{1,0:T(8,128)(2,1)S(1)} %reduce_sum.160, bf16[1024,192]{1,0:T(8,128)(2,1)} %get-tuple-element.29, bf16[384]{0:T(512)(128)(2,1)S(1)} %pad.9.clone), kind=kOutput, calls=%fused_computation.13 | convolution fusion | flops 1211891712 | bytes 4981504 | tf_op jit(solution)/shard_map/ti,di->td/dot_general | solution.py:499
  377.7 1.6 convolution_convert_fusion.4
  380.4 1.5 concatenate.47
  381.8 3.7 fusion.29
  386.5 2.3 copy.122
  388.9 3.0 maximum_maximum_fusion
  391.9 9.5 %all-to-all-done.7 = bf16[16,24,1536]{2,1,0:T(8,128)(2,1)S(1)} async-done(((bf16[16,24,1536]{2,1,0:T(8,128)(2,1)}), bf16[16,24,1536]{2,1,0:T(8,128)(2,1)S(1)}, u32[]{:S(2)}, u32[]{:S(2)}) %all-to-all-start.7) | async-done | bytes 1179680 | tf_op jit(solution)/shard_map/y_send/all_to_all | solution.py:331
  402.4 7.1 %all-to-all-start.9 = ((bf16[32,48,384]{2,1,0:T(8,128)(2,1)}), bf16[32,48,384]{2,1,0:T(8,128)(2,1)S(1)}, u32[]{:S(2)}, u32[]{:S(2)}) async-start(bf16[32,48,384]{2,1,0:T(8,128)(2,1)} %maximum_maximum_fusion), calls=%async_computation.10 | async-start | bytes 2359296 | tf_op jit(solution)/shard_map/grad_send/all_to_all | solution.py:496
  411.5 5.1 %convolution_bitcast_fusion.1 = f32[1,1536,512]{2,1,0:T(8,128)} fusion(bf16[768,1536]{1,0:T(8,128)(2,1)} %copy-done.11, bf16[768,512]{0,1:T(8,128)(2,1)} %copy-done.23), kind=kOutput, calls=%fused_computation.15 | convolution fusion | flops 1207959552 | bytes 6291456 | tf_op jit(solution)/shard_map/expert_grads/rd,rf->df/dot_general | solution.py:430
  416.7 3.1 convolution_bitcast_fusion.2
  419.9 4.6 convolution_bitcast_fusion
  424.5 1.2 fusion.14
  425.7 15.2 %all-to-all-done.9 = bf16[32,48,384]{2,1,0:T(8,128)(2,1)S(1)} async-done(((bf16[32,48,384]{2,1,0:T(8,128)(2,1)}), bf16[32,48,384]{2,1,0:T(8,128)(2,1)S(1)}, u32[]{:S(2)}, u32[]{:S(2)}) %all-to-all-start.9) | async-done | bytes 1179680 | tf_op jit(solution)/shard_map/grad_send/all_to_all | solution.py:496
  440.9 1.6 slice.156
  442.5 1.9 reduce_sum.163
  445.4 1.8 reshape.260
  451.6 1.6 convert_element_type.243
  453.2 13.6 %reduce-scatter.3.cloned.1.call-done = bf16[128,1536]{1,0:T(8,128)(2,1)} async-done(((bf16[1024,1536]{1,0:T(8,128)(2,1)}), bf16[128,1536]{1,0:T(8,128)(2,1)}) %reduce-scatter.3.cloned.1.call-update) | async-done | bytes 393232 | tf_op jit(solution)/shard_map/d_normed/reduce_scatter | solution.py:501
  466.8 1.3 fusion.32
  468.1 2.0 fusion.35
  (224 shorter events, 33.1 us)
Async XLA Ops:
  7.2 215.2 %copy-start = (bf16[1,512,1536]{2,1,0:T(8,128)(2,1)S(1)}, bf16[1,512,1536]{2,1,0:T(8,128)(2,1)}, u32[]{:S(2)}) copy-start(bf16[1,512,1536]{2,1,0:T(8,128)(2,1)} %param.26) | copy-start | bytes 4718596
  7.2 7.1 %copy-start.46 = (bf16[48]{0:T(256)(128)(2,1)S(1)}, bf16[48]{0:T(256)(128)(2,1)}, u32[]{:S(2)}) copy-start(bf16[48]{0:T(256)(128)(2,1)} %param.22) | copy-start | bytes 292
  7.2 49.3 %all-gather.3.cloned.1.call-start = ((), (), s32[]{:S(2)}) async-start(), calls=%async_computation.12 | async-start | bytes 3538944 | tf_op jit(solution)/shard_map/all_gather | solution.py:286
  7.9 130.9 %all-gather.5.cloned.1.call-start = ((), (), s32[]{:S(2)}) async-start(), calls=%async_computation.13 | async-start | bytes 5271552 | tf_op jit(solution)/shard_map/all_gather | solution.py:296
  12.3 2.5 copy-start.14
  13.3 1.5 copy-start.21
  52.9 6.3 %copy-start.13 = (bf16[32,48,384]{2,1,0:T(8,128)(2,1)}, bf16[32,48,384]{2,1,0:T(8,128)(2,1)S(1)}, u32[]{:S(2)}) copy-start(bf16[32,48,384]{2,1,0:T(8,128)(2,1)S(1)} %all_to_all.78) | copy-start | bytes 3538948
  56.5 2.8 copy-start.9
  59.3 1.9 copy-start.43
  62.2 5.4 %copy-start.36 = (s32[128,2]{0,1:T(2,128)S(1)}, s32[128,2]{0,1:T(2,128)}, u32[]{:S(2)}) copy-start(s32[128,2]{0,1:T(2,128)} %param.16) | copy-start | bytes 3076
  62.2 5.8 %copy-start.44 = (s32[12]{0:T(128)S(1)}, s32[12]{0:T(128)}, u32[]{:S(2)}) copy-start(s32[12]{0:T(128)} %lengths_ref.3) | copy-start | bytes 148
  63.3 9.4 %copy-start.16 = (bf16[128,1536]{1,0:T(8,128)(2,1)S(1)}, bf16[128,1536]{1,0:T(8,128)(2,1)}, u32[]{:S(2)}) copy-start(bf16[128,1536]{1,0:T(8,128)(2,1)} %param.27) | copy-start | bytes 1179652
  63.3 33.9 %all-to-all-start.1 = ((bf16[4,1024,128]{2,1,0:T(8,128)(2,1)}), bf16[4,1024,128]{2,1,0:T(8,128)(2,1)S(1)}, u32[]{:S(2)}, u32[]{:S(2)}) async-start(bf16[4,1024,128]{2,1,0:T(8,128)(2,1)} %broadcast_in_dim.153), calls=%async_computation.1 | async-start | bytes 2097152 | tf_op jit(solution)/shard_map/kv_send/all_to_all | solution.py:358
  72.3 1.9 copy-start.26
  72.6 199.4 %copy-start.32 = (s32[128]{0:T(128)}, s32[128]{0:T(128)S(1)}, u32[]{:S(2)}) copy-start(s32[128]{0:T(128)S(1)} %get-tuple-element.72) | copy-start | bytes 1540
  72.6 199.4 %copy-start.34 = (s32[128]{0:T(128)}, s32[128]{0:T(128)S(1)}, u32[]{:S(2)}) copy-start(s32[128]{0:T(128)S(1)} %get-tuple-element.73) | copy-start | bytes 1540
  98.1 40.7 %copy-start.6 = (bf16[128,1536]{1,0:T(8,128)(2,1)S(1)}, bf16[128,1536]{1,0:T(8,128)(2,1)}, u32[]{:S(2)}) copy-start(bf16[128,1536]{1,0:T(8,128)(2,1)} %param.14) | copy-start | bytes 1179652
  115.1 15.7 %all-to-all-start.2 = ((bf16[8,128,192]{1,2,0:T(8,128)(2,1)}), bf16[8,128,192]{1,2,0:T(8,128)(2,1)S(1)}, u32[]{:S(2)}, u32[]{:S(2)}) async-start(bf16[8,128,192]{1,2,0:T(8,128)(2,1)} %copy.116), calls=%async_computation.2 | async-start | bytes 786432 | tf_op jit(solution)/shard_map/all_to_all | solution.py:372
  130.8 11.3 %copy-start.10 = (bf16[8,128,192]{1,2,0:T(8,128)(2,1)}, bf16[8,128,192]{1,2,0:T(8,128)(2,1)S(1)}, u32[]{:S(2)}) copy-start(bf16[8,128,192]{1,2,0:T(8,128)(2,1)S(1)} %all-to-all-done.2) | copy-start | bytes 1179652
  142.1 1.5 copy-start.51
  142.1 130.8 %copy-start.37 = (f32[128]{0:T(128)}, f32[128]{0:T(128)S(1)}, u32[]{:S(2)}) copy-start(f32[128]{0:T(128)S(1)} %add_rsqrt_fusion.2) | copy-start | bytes 1540
  143.6 4.3 copy-start.7
  185.1 30.3 %all-to-all-start.4 = ((bf16[16,24,1536]{2,1,0:T(8,128)(2,1)}), bf16[16,24,1536]{2,1,0:T(8,128)(2,1)}, u32[]{:S(2)}, u32[]{:S(2)}) async-start(bf16[16,24,1536]{2,1,0:T(8,128)(2,1)} %bitcast.21), calls=%async_computation.4 | async-start | bytes 2359296 | tf_op jit(solution)/shard_map/d_send/all_to_all | solution.py:331
  189.7 25.8 %collective-permute-start = (bf16[384,1664]{1,0:T(8,128)(2,1)}, bf16[384,1664]{1,0:T(8,128)(2,1)}, u32[]{:S(2)}, u32[]{:S(2)}) collective-permute-start(bf16[384,1664]{1,0:T(8,128)(2,1)} %bitcast.99), channel_id=1, source_target_pairs={{0,16},{16,0},{1,17},{17,1},{2,18},{18,2},{3,19},{19,3},{4,20},{20... | collective-permute-start | bytes 3833864 | tf_op jit(solution)/shard_map/ppermute | solution.py:340
  215.4 6.9 %collective-permute-start.2 = (bf16[384,1536]{1,0:T(8,128)(2,1)}, bf16[384,1536]{1,0:T(8,128)(2,1)S(1)}, u32[]{:S(2)}, u32[]{:S(2)}) collective-permute-start(bf16[384,1536]{1,0:T(8,128)(2,1)} %bitcast.22), channel_id=1, source_target_pairs={{0,16},{16,0},{1,17},{17,1},{2,18},{18,2},{3,19},{19,3},{4,20},{20... | collective-permute-start | bytes 3538952 | tf_op jit(solution)/shard_map/d_swap/ppermute | solution.py:340
  216.8 5.5 %copy-start.40 = (f32[768]{0:T(1024)}, f32[768]{0:T(1024)S(1)}, u32[]{:S(2)}) copy-start(f32[768]{0:T(1024)S(1)} %select_reduce_fusion) | copy-start | bytes 9220
  216.8 1.8 copy-start.18
  218.6 1.5 copy-start.11
  218.6 2.3 copy-start.48
  220.9 1.5 copy-start.55
  222.4 4.2 copy-start.57
  222.4 4.2 copy-start.49
  226.6 1.5 copy-start.53
  229.7 3.4 collective-permute-start.3
  230.3 2.5 collective-permute-start.4
  233.1 39.8 %slice-start = ((s8[5111808]{0:T(1024)(128)(4,1)}), s8[917504]{0:T(1024)(128)(4,1)S(1)}, s32[]{:S(2)}) async-start(s8[5111808]{0:T(1024)(128)(4,1)} %bitcast.127), calls=%async_computation.16 | async-start | bytes 1835008
  233.5 39.4 %slice-start.1 = ((s8[5111808]{0:T(1024)(128)(4,1)}), s8[4194304]{0:T(1024)(128)(4,1)S(1)}, s32[]{:S(2)}) async-start(s8[5111808]{0:T(1024)(128)(4,1)} %bitcast.127), calls=%async_computation.17 | async-start | bytes 8388608
  279.1 11.9 %all-to-all-start.6 = ((bf16[128,8,192]{0,2,1:T(8,128)(2,1)}), bf16[128,8,192]{0,2,1:T(8,128)(2,1)}, u32[]{:S(2)}, u32[]{:S(2)}) async-start(bf16[128,8,192]{0,2,1:T(8,128)(2,1)} %bitcast.121), calls=%async_computation.6 | async-start | bytes 786432 | tf_op jit(solution)/shard_map/all_to_all | solution.py:458
  283.2 168.3 %reduce-scatter.5.cloned.1.call-start = ((), (), s32[]{:S(2)}) async-start(), calls=%async_computation.15 | async-start | bytes 4866048 | tf_op jit(solution)/shard_map/grad_out/reduce_scatter | solution.py:464
  297.2 3.1 collective-permute-start.1
  366.3 35.1 %all-to-all-start.7 = ((bf16[16,24,1536]{2,1,0:T(8,128)(2,1)}), bf16[16,24,1536]{2,1,0:T(8,128)(2,1)S(1)}, u32[]{:S(2)}, u32[]{:S(2)}) async-start(bf16[16,24,1536]{2,1,0:T(8,128)(2,1)} %bitcast.113), calls=%async_computation.7 | async-start | bytes 2359296 | tf_op jit(solution)/shard_map/y_send/all_to_all | solution.py:331
  370.0 96.8 %reduce-scatter.3.cloned.1.call-start = ((), (), s32[]{:S(2)}) async-start(), calls=%async_computation.14 | async-start | bytes 3538944 | tf_op jit(solution)/shard_map/d_normed/reduce_scatter | solution.py:501
  370.1 6.6 %copy-start.45 = (bf16[384]{0:T(512)(128)(2,1)}, bf16[384]{0:T(512)(128)(2,1)S(1)}, u32[]{:S(2)}) copy-start(bf16[384]{0:T(512)(128)(2,1)S(1)} %pad.9.clone) | copy-start | bytes 2308
  371.6 5.1 %copy-start.30 = (bf16[1024,128]{1,0:T(8,128)(2,1)}, bf16[1024,128]{1,0:T(8,128)(2,1)S(1)}, u32[]{:S(2)}) copy-start(bf16[1024,128]{1,0:T(8,128)(2,1)S(1)} %reduce_sum.160) | copy-start | bytes 786436
  376.7 3.6 copy-start.31
  391.9 17.6 %copy-start.15 = (bf16[48,8,192]{2,1,0:T(8,128)(2,1)S(1)}, bf16[48,8,192]{2,1,0:T(8,128)(2,1)}, u32[]{:S(2)}) copy-start(bf16[48,8,192]{2,1,0:T(8,128)(2,1)} %copy-done.14) | copy-start | bytes 442372
  391.9 18.3 %copy-start.22 = (bf16[48,8,64]{2,1,0:T(8,128)(2,1)S(1)}, bf16[48,8,64]{2,1,0:T(8,128)(2,1)}, u32[]{:S(2)}) copy-start(bf16[48,8,64]{2,1,0:T(8,128)(2,1)} %copy-done.21) | copy-start | bytes 147460
  391.9 19.0 %copy-start.20 = (bf16[48,8,64]{2,1,0:T(8,128)(2,1)S(1)}, bf16[48,8,64]{2,1,0:T(8,128)(2,1)}, u32[]{:S(2)}) copy-start(bf16[48,8,64]{2,1,0:T(8,128)(2,1)} %copy-done.19) | copy-start | bytes 147460
  402.4 38.5 %all-to-all-start.9 = ((bf16[32,48,384]{2,1,0:T(8,128)(2,1)}), bf16[32,48,384]{2,1,0:T(8,128)(2,1)S(1)}, u32[]{:S(2)}, u32[]{:S(2)}) async-start(bf16[32,48,384]{2,1,0:T(8,128)(2,1)} %maximum_maximum_fusion), calls=%async_computation.10 | async-start | bytes 2359296 | tf_op jit(solution)/shard_map/grad_send/all_to_all | solution.py:496
  411.5 5.1 %copy-start.12 = (bf16[768,1536]{1,0:T(8,128)(2,1)S(1)}, bf16[768,1536]{1,0:T(8,128)(2,1)}, u32[]{:S(2)}) copy-start(bf16[768,1536]{1,0:T(8,128)(2,1)} %copy-done.11) | copy-start | bytes 7077892
  411.5 5.1 %copy-start.54 = (bf16[768,512]{0,1:T(8,128)(2,1)S(1)}, bf16[768,512]{0,1:T(8,128)(2,1)}, u32[]{:S(2)}) copy-start(bf16[768,512]{0,1:T(8,128)(2,1)} %copy-done.53) | copy-start | bytes 2359300
  416.7 3.2 copy-start.42
  416.7 3.2 copy-start.50
  416.7 3.2 copy-start.56
  416.7 3.1 copy-start.58
  419.8 4.7 copy-start.5
  419.9 4.7 copy-start.33
  419.9 4.7 copy-start.35
  419.9 4.7 copy-start.39
  448.9 1.8 copy-start.24
  449.0 1.8 copy-start.27
  449.0 1.8 copy-start.28
  449.1 1.9 copy-start.47
  451.0 19.0 %copy-start.1 = (bf16[1,512,1536]{2,1,0:T(8,128)(2,1)S(1)}, bf16[1,512,1536]{2,1,0:T(8,128)(2,1)}, u32[]{:S(2)}) copy-start(bf16[1,512,1536]{2,1,0:T(8,128)(2,1)} %param.26) | copy-start | bytes 4718596
  (12 other events, 13.4 us)
Sparse Core Ops, SparseCore 0:
  9.9 46.5 all-gather.2
  59.9 78.8 all-gather.4
  293.2 123.4 reduce-scatter.4
  419.9 46.8 reduce-scatter.2
